TPU v7x, 512 devices: a whole 4x8x8 slice. The times are simulated.
512 devices in a mesh: seq: 64 (over x, z, core), blk: 8 (over y).
Axes of the slice: x: 4, y: 8, z: 8, core: 2. Of those that a mesh axis runs over, the one named last changes fastest.
Arguments:
- query_states: bfloat16 [65536, 2048], P(('seq', 'blk')), may hold values from -6 to 6
- key_states: bfloat16 [65536, 2048], P(('seq', 'blk')), may hold values from -6 to 6
- value_states: bfloat16 [65536, 2048], P(('seq', 'blk')), may hold values from -6 to 6
- output_grad: bfloat16 [65536, 2048], P(('seq', 'blk')), may hold values from -6 to 6
- near_mask: int32 [512, 2], replicated, may hold values 0 or 1
- motion_count: int32 [512], replicated, may hold values from 0 to 3
Outputs:
- query_grad: bfloat16 [65536, 2048], P(('seq', 'blk'))
- key_grad: bfloat16 [65536, 2048], P(('seq', 'blk'))
- value_grad: bfloat16 [65536, 2048], P(('seq', 'blk'))
All inputs are finite; a program needn't handle non-finite values.
Results may differ from a plain program's by a relative error of at most 0.012.
Values may be sent and summed in bfloat16 or wider, within the bound.
No kernel may reach another device: no remote copies, remote signals or barrier semaphores. Data moves between devices by JAX's collectives and lax.ppermute only.
A program may use at most 64 MiB of HBM per device.

v0:
```python
import jax
import jax.numpy as jnp
from jax import lax
from jax.experimental import pallas as pl
from jax.experimental.pallas import tpu as pltpu
from jax.sharding import PartitionSpec as P


HEAD_DIM = 64
TILE = 128
REACH = 2
LANES = 128
CHUNKS = 2
WINDOW = 2 * REACH + 1
SPAN = WINDOW * TILE
NT = (((1,), (1,)), ((), ()))
TN = (((0,), (0,)), ((), ()))


def cost(flops, moved, exps=0):
    return pl.CostEstimate(flops=flops, bytes_accessed=moved, transcendentals=exps)


def pack(arrays, chunk, peers, after=()):
    rows, count = arrays[0].shape[0], len(arrays)

    def body(*refs):
        ins, refs = refs[:count], refs[count + len(after):]
        out_ref, held, in_sem, out_sem = refs
        reads = [
            [
                pltpu.make_async_copy(
                    ins[n].at[:, pl.ds((chunk * peers + b) * LANES, LANES)], held.at[b, n], in_sem.at[b, n])
                for n in range(count)
            ]
            for b in range(peers)
        ]
        writes = [pltpu.make_async_copy(held.at[b], out_ref.at[b], out_sem.at[b]) for b in range(peers)]
        for b in range(peers):
            for n in range(count):
                reads[b][n].start()
        for b in range(peers):
            for n in range(count):
                reads[b][n].wait()
            writes[b].start()
        for b in range(peers):
            writes[b].wait()

    shape = (peers, count, rows, LANES)
    return pl.pallas_call(
        body,
        in_specs=[pl.BlockSpec(memory_space=pl.ANY)] * (count + len(after)),
        out_specs=pl.BlockSpec(memory_space=pl.ANY),
        out_shape=jax.ShapeDtypeStruct(shape, jnp.bfloat16),
        scratch_shapes=[
            pltpu.VMEM(shape, jnp.bfloat16),
            pltpu.SemaphoreType.DMA((peers, count)),
            pltpu.SemaphoreType.DMA((peers,)),
        ],
        cost_estimate=cost(0, 2 * peers * count * rows * LANES * 2),
        name="pack",
    )(*arrays, *after)


def unpack(grads, chunk, columns, so_far=None):
    peers, count, rows, _ = grads.shape
    given = [] if so_far is None else list(so_far)

    def body(in_ref, *refs):
        outs = refs[len(given):len(given) + count]
        held, in_sem, out_sem = refs[len(given) + count:]
        reads = [pltpu.make_async_copy(in_ref.at[b], held.at[b], in_sem.at[b]) for b in range(peers)]
        writes = [
            [
                pltpu.make_async_copy(
                    held.at[b, n], outs[n].at[:, pl.ds((chunk * peers + b) * LANES, LANES)], out_sem.at[b, n])
                for n in range(count)
            ]
            for b in range(peers)
        ]
        for b in range(peers):
            reads[b].start()
        for b in range(peers):
            reads[b].wait()
            for n in range(count):
                writes[b][n].start()
        for b in range(peers):
            for n in range(count):
                writes[b][n].wait()

    hbm = pl.BlockSpec(memory_space=pl.ANY)
    return pl.pallas_call(
        body,
        in_specs=[hbm] * (1 + len(given)),
        out_specs=[hbm] * count,
        out_shape=[jax.ShapeDtypeStruct((rows, columns), jnp.bfloat16)] * count,
        scratch_shapes=[
            pltpu.VMEM(grads.shape, jnp.bfloat16),
            pltpu.SemaphoreType.DMA((peers,)),
            pltpu.SemaphoreType.DMA((peers, count)),
        ],
        input_output_aliases={1 + n: n for n in range(len(given))},
        compiler_params=pltpu.CompilerParams(vmem_limit_bytes=4 << 20),
        cost_estimate=cost(0, 2 * peers * count * rows * LANES * 2),
        name="unpack",
    )(grads, *given)


def rim_body(x_ref, low_ref, high_ref):
    tiles = x_ref.shape[0]
    deep = 2 * REACH
    for ref, wide, narrow in ((low_ref, 0, 0), (high_ref, tiles - deep, tiles - REACH)):
        for t in range(deep):
            ref[t] = x_ref[wide + t, 1]
            ref[deep + t] = x_ref[wide + t, 2]
        for t in range(REACH):
            ref[2 * deep + t] = x_ref[narrow + t, 0]
            ref[2 * deep + REACH + t] = x_ref[narrow + t, 3]


def rims(taken):
    shape = jax.ShapeDtypeStruct((6 * REACH,) + taken.shape[2:], taken.dtype)
    vmem = pl.BlockSpec(memory_space=pltpu.VMEM)
    return pl.pallas_call(
        rim_body,
        in_specs=[vmem],
        out_specs=[vmem] * 2,
        out_shape=[shape] * 2,
        compiler_params=pltpu.CompilerParams(vmem_limit_bytes=8 << 20),
        cost_estimate=cost(0, 2 << 20),
        name="rims",
    )(taken)


def attend_body(bias_ref, x_ref, left_ref, right_ref, out_ref, key_ref, value_ref, dkey_ref, dvalue_ref):
    tiles = x_ref.shape[0]
    deep = 2 * REACH
    for n, ref in ((0, key_ref), (1, value_ref)):
        for t in range(deep):
            ref[t * TILE:(t + 1) * TILE] = left_ref[n * deep + t]
            at = (deep + tiles + t) * TILE
            ref[at:at + TILE] = right_ref[n * deep + t]
        for t in range(tiles):
            ref[(deep + t) * TILE:(deep + t + 1) * TILE] = x_ref[t, 1 + n]
    dkey_ref[...] = jnp.zeros_like(dkey_ref)
    dvalue_ref[...] = jnp.zeros_like(dvalue_ref)
    first = lax.broadcasted_iota(jnp.int32, (TILE, LANES), 1) < HEAD_DIM
    scale = float(HEAD_DIM) ** (-0.5)

    def both_heads(block):
        zero = jnp.zeros_like(block)
        return jnp.concatenate([jnp.where(first, block, zero), jnp.where(first, zero, block)], axis=0)

    def scores_of(i, query_tile, grad_tile):
        at = i * TILE if isinstance(i, int) else pl.multiple_of(i * TILE, TILE)
        query = both_heads(query_tile * jnp.bfloat16(scale))
        grad = both_heads(grad_tile)
        key = key_ref[pl.ds(at, SPAN)]
        value = value_ref[pl.ds(at, SPAN)]
        scores = lax.dot_general(key, query, NT, preferred_element_type=jnp.float32)
        scores = jnp.concatenate(
            [scores[t * TILE:(t + 1) * TILE] + bias_ref[i * WINDOW + t] for t in range(WINDOW)], axis=0)
        top = jnp.max(scores, axis=0, keepdims=True)
        weights = jnp.exp(scores - top)
        probs = weights * (1.0 / jnp.sum(weights, axis=0, keepdims=True))
        probs_b = probs.astype(jnp.bfloat16)
        dprobs = lax.dot_general(value, grad, NT, preferred_element_type=jnp.float32)
        delta = jnp.sum(probs_b.astype(jnp.float32) * dprobs, axis=0, keepdims=True)
        return query, grad, key, probs, probs_b, dprobs, delta

    def near(i, query_tile, grad_tile):
        query, grad, _, probs, probs_b, dprobs, delta = scores_of(i, query_tile, grad_tile)
        low, high = max(0, deep - i), min(WINDOW, deep + tiles - i)
        rows = slice(low * TILE, high * TILE)
        dscores = (probs[rows] * (dprobs[rows] - delta)).astype(jnp.bfloat16)
        at = slice((i + low - REACH) * TILE, (i + high - REACH) * TILE)
        dkey_ref[at] += jnp.dot(dscores, query, preferred_element_type=jnp.float32)
        dvalue_ref[at] += jnp.dot(probs_b[rows], grad, preferred_element_type=jnp.float32)

    def step(t):
        query, grad, key, probs, probs_b, dprobs, delta = scores_of(t + REACH, x_ref[t, 0], x_ref[t, 3])
        dscores = (probs * (dprobs - delta)).astype(jnp.bfloat16)
        at = pl.multiple_of(t * TILE, TILE)
        dkey_ref[pl.ds(at, SPAN)] += jnp.dot(dscores, query, preferred_element_type=jnp.float32)
        dvalue_ref[pl.ds(at, SPAN)] += jnp.dot(probs_b, grad, preferred_element_type=jnp.float32)
        dquery = lax.dot_general(dscores, key, TN, preferred_element_type=jnp.float32)
        out_ref[t, 0] = (jnp.where(first, dquery[:TILE], dquery[TILE:]) * scale).astype(jnp.bfloat16)

    def steps(i, _):
        step(2 * i)
        step(2 * i + 1)
        return 0

    lax.fori_loop(0, tiles // 2, steps, 0)
    for t in range(REACH):
        near(t, left_ref[2 * deep + t], left_ref[2 * deep + REACH + t])
        near(REACH + tiles + t, right_ref[2 * deep + t], right_ref[2 * deep + REACH + t])
    for n, ref in ((0, dkey_ref), (1, dvalue_ref)):
        for t in range(tiles):
            out_ref[t, 1 + n] = ref[(REACH + t) * TILE:(REACH + t + 1) * TILE].astype(jnp.bfloat16)


def attend(bias, taken, left, right):
    tiles = taken.shape[0]
    wide = (tiles + 4 * REACH) * TILE
    vmem = pl.BlockSpec(memory_space=pltpu.VMEM)
    pairs = (tiles + 2 * REACH) * WINDOW * 2
    return pl.pallas_call(
        attend_body,
        in_specs=[pl.BlockSpec(memory_space=pltpu.SMEM), vmem, vmem, vmem],
        out_specs=vmem,
        out_shape=jax.ShapeDtypeStruct((tiles, 3, TILE, LANES), jnp.bfloat16),
        scratch_shapes=[pltpu.VMEM((wide, LANES), jnp.bfloat16)] * 2
        + [pltpu.VMEM(((tiles + 2 * REACH) * TILE, LANES), jnp.float32)] * 2,
        compiler_params=pltpu.CompilerParams(vmem_limit_bytes=32 << 20),
        cost_estimate=cost(pairs * 5 * 2 * TILE * TILE * HEAD_DIM * 8, 3 << 20, pairs * TILE * TILE),
        name="attend",
    )(bias, taken, left, right)


def tile_bias(near_mask, motion_count, tiles):
    first = lax.axis_index("seq") * tiles
    total = near_mask.shape[0]
    near = lax.dynamic_slice_in_dim(jnp.pad(near_mask, ((REACH, REACH), (0, 0))), first, tiles + 2 * REACH, 0) == 1
    far = lax.dynamic_slice_in_dim(jnp.pad(motion_count, (REACH, REACH)), first, tiles + 2 * REACH, 0) >= 2
    own = jnp.ones_like(far)
    allowed = jnp.stack([far, near[:, 0], own, near[:, 1], far], axis=1)
    index = first - REACH + jnp.arange(tiles + 2 * REACH)
    others = index[:, None] + jnp.arange(-REACH, REACH + 1)[None, :]
    allowed &= (others >= 0) & (others < total)
    return jnp.where(allowed, 0.0, -1e30).astype(jnp.float32).reshape(-1)


def per_device(query_states, key_states, value_states, output_grad, near_mask, motion_count):
    peers, groups = lax.axis_size("blk"), lax.axis_size("seq")
    up = [(i, i + 1) for i in range(groups - 1)]
    down = [(j, i) for i, j in up]
    arrays = (query_states, key_states, value_states, output_grad)
    bias = tile_bias(near_mask, motion_count, peers)

    taken, results = [], None
    for c in range(CHUNKS):
        packed = pack(arrays, c, peers, (bias,) if c else ())
        taken.append(lax.all_to_all(packed, "blk", split_axis=0, concat_axis=0, tiled=True))
    for c in range(CHUNKS):
        low, high = rims(taken[c])
        left = lax.ppermute(high, "seq", up)
        right = lax.ppermute(low, "seq", down)
        out = attend(bias, taken[c], left, right)
        back = lax.all_to_all(out, "blk", split_axis=0, concat_axis=0, tiled=True)
        results = unpack(back, c, query_states.shape[1], results)
    return tuple(results)


def solution(mesh):
    spec = P(("seq", "blk"), None)
    return jax.shard_map(
        per_device, mesh=mesh, in_specs=(spec,) * 4 + (P(), P()), out_specs=(spec,) * 3, check_vma=False
    )
```

profile of v0, /device:TPU:6, one launch (start us, length us, event | category | flops | bytes accessed | tf_op | source)
XLA Modules:
  0.0 132.3 jit_solution(166428743637164336)
XLA Ops:
  0.6 2.2 %pack.3 = bf16[8,4,128,128]{3,2,1,0:T(8,128)(2,1)} custom-call(bf16[128,2048]{1,0:T(8,128)(2,1)} %refs_0_.3, bf16[128,2048]{1,0:T(8,128)(2,1)} %refs_1_.3, bf16[128,2048]{1,0:T(8,128)(2,1)} %refs_2_.3, bf16[128,2048]{1,0:T(8,128)(2,1)} %refs_3_.3), custom_call_target="tpu_custom_call" | custom-call | bytes 2097152 | tf_op jit(solution)/shard_map/pack/pallas_call | solution.py:50
  2.9 7.1 %all-to-all-start.2 = ((bf16[8,4,128,128]{3,2,1,0:T(8,128)(2,1)}), bf16[8,4,128,128]{3,2,1,0:T(8,128)(2,1)S(1)}, u32[]{:S(2)}, u32[]{:S(2)}) async-start(bf16[8,4,128,128]{3,2,1,0:T(8,128)(2,1)} %pack.3), calls=%async_computation.2 | async-start | bytes 2097152 | tf_op jit(solution)/shard_map/all_to_all | solution.py:244
  10.0 0.0 copy-start.1
  10.0 0.7 copy-done.1
  10.7 0.0 copy-start.2
  10.7 0.1 fusion.3
  10.7 0.6 copy-done.2
  11.3 0.1 compare_bitcast_fusion
  11.5 0.1 fusion.2
  11.6 0.1 copy.13
  11.7 0.6 reshape.27.refs_4_.bias_ref
  12.3 2.2 %pack.2 = bf16[8,4,128,128]{3,2,1,0:T(8,128)(2,1)} custom-call(bf16[128,2048]{1,0:T(8,128)(2,1)} %refs_0_.3, bf16[128,2048]{1,0:T(8,128)(2,1)} %refs_1_.3, bf16[128,2048]{1,0:T(8,128)(2,1)} %refs_2_.3, bf16[128,2048]{1,0:T(8,128)(2,1)} %refs_3_.3, f32[60]{0:T(128)} %reshape.27.refs_4_.bias_ref), custom_call_target="tpu_custom_call" | custom-call | bytes 2097152 | tf_op jit(solution)/shard_map/pack/pallas_call | solution.py:50
  14.5 24.2 %all-to-all-done.2.x_ref = bf16[8,4,128,128]{3,2,1,0:T(8,128)(2,1)S(1)} async-done(((bf16[8,4,128,128]{3,2,1,0:T(8,128)(2,1)}), bf16[8,4,128,128]{3,2,1,0:T(8,128)(2,1)S(1)}, u32[]{:S(2)}, u32[]{:S(2)}) %all-to-all-start.2) | async-done | bytes 1048608 | tf_op jit(solution)/shard_map/all_to_all | solution.py:244
  38.7 3.6 %all-to-all-start = ((bf16[8,4,128,128]{3,2,1,0:T(8,128)(2,1)}), bf16[8,4,128,128]{3,2,1,0:T(8,128)(2,1)S(1)}, u32[]{:S(2)}, u32[]{:S(2)}) async-start(bf16[8,4,128,128]{3,2,1,0:T(8,128)(2,1)} %pack.2), calls=%async_computation | async-start | bytes 2097152 | tf_op jit(solution)/shard_map/all_to_all | solution.py:244
  42.3 0.1 rims.3
  42.3 0.0 copy-start
  42.3 1.9 %collective-permute-start.2 = (bf16[12,128,128]{2,1,0:T(8,128)(2,1)S(1)}, bf16[12,128,128]{2,1,0:T(8,128)(2,1)S(1)}, u32[]{:S(2)}, u32[]{:S(2)}) collective-permute-start(bf16[12,128,128]{2,1,0:T(8,128)(2,1)S(1)} %get-tuple-element.12), channel_id=1, source_target_pairs={{0,8},{8,16},{16,24},{24,32},{32,40},{40,48},{48,56},{56,64},{64,7... | collective-permute-start | bytes 1179656 | tf_op jit(solution)/shard_map/ppermute | solution.py:247
  44.3 10.8 %collective-permute-start.3 = (bf16[12,128,128]{2,1,0:T(8,128)(2,1)S(1)}, bf16[12,128,128]{2,1,0:T(8,128)(2,1)S(1)}, u32[]{:S(2)}, u32[]{:S(2)}) collective-permute-start(bf16[12,128,128]{2,1,0:T(8,128)(2,1)S(1)} %get-tuple-element.13), channel_id=1, source_target_pairs={{8,0},{16,8},{24,16},{32,24},{40,32},{48,40},{56,48},{64,56},{72,6... | collective-permute-start | bytes 1179656 | tf_op jit(solution)/shard_map/ppermute | solution.py:248
  55.1 3.5 %collective-permute-done.2.left_ref = bf16[12,128,128]{2,1,0:T(8,128)(2,1)S(1)} collective-permute-done((bf16[12,128,128]{2,1,0:T(8,128)(2,1)S(1)}, bf16[12,128,128]{2,1,0:T(8,128)(2,1)S(1)}, u32[]{:S(2)}, u32[]{:S(2)}) %collective-permute-start.2) | collective-permute-done | bytes 393248 | tf_op jit(solution)/shard_map/ppermute | solution.py:247
  58.6 1.8 %collective-permute-done.3.right_ref = bf16[12,128,128]{2,1,0:T(8,128)(2,1)S(1)} collective-permute-done((bf16[12,128,128]{2,1,0:T(8,128)(2,1)S(1)}, bf16[12,128,128]{2,1,0:T(8,128)(2,1)S(1)}, u32[]{:S(2)}, u32[]{:S(2)}) %collective-permute-start.3) | collective-permute-done | bytes 393248 | tf_op jit(solution)/shard_map/ppermute | solution.py:248
  60.4 0.0 copy-done
  60.4 11.0 %attend.3 = bf16[8,3,128,128]{3,2,1,0:T(8,128)(2,1)} custom-call(f32[60]{0:T(128)S(1)} %copy-done, bf16[8,4,128,128]{3,2,1,0:T(8,128)(2,1)S(1)} %all-to-all-done.2.x_ref, bf16[12,128,128]{2,1,0:T(8,128)(2,1)S(1)} %collective-permute-done.2.left_ref, bf16[12,128,128]{2,1,0:T(8,128)(2,1)S(1)} %collective-permute-done.3.right_ref), custom_call_target="tpu_custom_call" | custom-call | flops 10066329600 | bytes 3145728 | tf_op jit(solution)/shard_map/attend/pallas_call | solution.py:208
  71.3 0.1 all-to-all-done.x_ref
  71.4 6.8 %all-to-all-start.3 = ((bf16[8,3,128,128]{3,2,1,0:T(8,128)(2,1)}), bf16[8,3,128,128]{3,2,1,0:T(8,128)(2,1)S(1)}, u32[]{:S(2)}, u32[]{:S(2)}) async-start(bf16[8,3,128,128]{3,2,1,0:T(8,128)(2,1)} %attend.3), calls=%async_computation.3 | async-start | bytes 1572864 | tf_op jit(solution)/shard_map/all_to_all | solution.py:250
  78.2 0.1 rims.2
  78.2 1.9 %collective-permute-start = (bf16[12,128,128]{2,1,0:T(8,128)(2,1)S(1)}, bf16[12,128,128]{2,1,0:T(8,128)(2,1)S(1)}, u32[]{:S(2)}, u32[]{:S(2)}) collective-permute-start(bf16[12,128,128]{2,1,0:T(8,128)(2,1)S(1)} %get-tuple-element.10), channel_id=1, source_target_pairs={{0,8},{8,16},{16,24},{24,32},{32,40},{40,48},{48,56},{56,64},{64,7... | collective-permute-start | bytes 1179656 | tf_op jit(solution)/shard_map/ppermute | solution.py:247
  80.2 7.6 %collective-permute-start.1 = (bf16[12,128,128]{2,1,0:T(8,128)(2,1)S(1)}, bf16[12,128,128]{2,1,0:T(8,128)(2,1)S(1)}, u32[]{:S(2)}, u32[]{:S(2)}) collective-permute-start(bf16[12,128,128]{2,1,0:T(8,128)(2,1)S(1)} %get-tuple-element.11), channel_id=1, source_target_pairs={{8,0},{16,8},{24,16},{32,24},{40,32},{48,40},{56,48},{64,56},{72,6... | collective-permute-start | bytes 1179656 | tf_op jit(solution)/shard_map/ppermute | solution.py:248
  87.8 3.5 %collective-permute-done.left_ref = bf16[12,128,128]{2,1,0:T(8,128)(2,1)S(1)} collective-permute-done((bf16[12,128,128]{2,1,0:T(8,128)(2,1)S(1)}, bf16[12,128,128]{2,1,0:T(8,128)(2,1)S(1)}, u32[]{:S(2)}, u32[]{:S(2)}) %collective-permute-start) | collective-permute-done | bytes 393248 | tf_op jit(solution)/shard_map/ppermute | solution.py:247
  91.3 1.8 %collective-permute-done.1.right_ref = bf16[12,128,128]{2,1,0:T(8,128)(2,1)S(1)} collective-permute-done((bf16[12,128,128]{2,1,0:T(8,128)(2,1)S(1)}, bf16[12,128,128]{2,1,0:T(8,128)(2,1)S(1)}, u32[]{:S(2)}, u32[]{:S(2)}) %collective-permute-start.1) | collective-permute-done | bytes 393248 | tf_op jit(solution)/shard_map/ppermute | solution.py:248
  93.1 10.9 %attend.2 = bf16[8,3,128,128]{3,2,1,0:T(8,128)(2,1)} custom-call(f32[60]{0:T(128)S(1)} %copy-done, bf16[8,4,128,128]{3,2,1,0:T(8,128)(2,1)S(1)} %all-to-all-done.x_ref, bf16[12,128,128]{2,1,0:T(8,128)(2,1)S(1)} %collective-permute-done.left_ref, bf16[12,128,128]{2,1,0:T(8,128)(2,1)S(1)} %collective-permute-done.1.right_ref), custom_call_target="tpu_custom_call" | custom-call | flops 10066329600 | bytes 3145728 | tf_op jit(solution)/shard_map/attend/pallas_call | solution.py:208
  104.0 0.0 all-to-all-done.3.in_ref
  104.0 6.8 %all-to-all-start.1 = ((bf16[8,3,128,128]{3,2,1,0:T(8,128)(2,1)}), bf16[8,3,128,128]{3,2,1,0:T(8,128)(2,1)S(1)}, u32[]{:S(2)}, u32[]{:S(2)}) async-start(bf16[8,3,128,128]{3,2,1,0:T(8,128)(2,1)} %attend.2), calls=%async_computation.1 | async-start | bytes 1572864 | tf_op jit(solution)/shard_map/all_to_all | solution.py:250
  110.8 2.2 %unpack.2 = (bf16[128,2048]{1,0:T(8,128)(2,1)}, bf16[128,2048]{1,0:T(8,128)(2,1)}, bf16[128,2048]{1,0:T(8,128)(2,1)}) custom-call(bf16[8,3,128,128]{3,2,1,0:T(8,128)(2,1)S(1)} %all-to-all-done.3.in_ref), custom_call_target="tpu_custom_call" | custom-call | bytes 1572864 | tf_op jit(solution)/shard_map/unpack/pallas_call | solution.py:92
  113.0 17.2 %all-to-all-done.1.in_ref = bf16[8,3,128,128]{3,2,1,0:T(8,128)(2,1)S(1)} async-done(((bf16[8,3,128,128]{3,2,1,0:T(8,128)(2,1)}), bf16[8,3,128,128]{3,2,1,0:T(8,128)(2,1)S(1)}, u32[]{:S(2)}, u32[]{:S(2)}) %all-to-all-start.1) | async-done | bytes 786464 | tf_op jit(solution)/shard_map/all_to_all | solution.py:250
  130.2 2.1 %unpack.3 = (bf16[128,2048]{1,0:T(8,128)(2,1)}, bf16[128,2048]{1,0:T(8,128)(2,1)}, bf16[128,2048]{1,0:T(8,128)(2,1)}) custom-call(bf16[8,3,128,128]{3,2,1,0:T(8,128)(2,1)S(1)} %all-to-all-done.1.in_ref, bf16[128,2048]{1,0:T(8,128)(2,1)} %get-tuple-element.14.refs_0_, ...), custom_call_target="tpu_custom_call", output_to_operand_aliasing={{0}: (1, {}), {1}: (2, {}), {2}: (3, {})} | custom-call | bytes 1572864 | tf_op jit(solution)/shard_map/unpack/pallas_call | solution.py:92
  (5 shorter events, 0.1 us)
Async XLA Ops:
  2.9 35.8 %all-to-all-start.2 = ((bf16[8,4,128,128]{3,2,1,0:T(8,128)(2,1)}), bf16[8,4,128,128]{3,2,1,0:T(8,128)(2,1)S(1)}, u32[]{:S(2)}, u32[]{:S(2)}) async-start(bf16[8,4,128,128]{3,2,1,0:T(8,128)(2,1)} %pack.3), calls=%async_computation.2 | async-start | bytes 2097152 | tf_op jit(solution)/shard_map/all_to_all | solution.py:244
  10.0 0.7 copy-start.1
  10.7 0.7 copy-start.2
  38.7 32.7 %all-to-all-start = ((bf16[8,4,128,128]{3,2,1,0:T(8,128)(2,1)}), bf16[8,4,128,128]{3,2,1,0:T(8,128)(2,1)S(1)}, u32[]{:S(2)}, u32[]{:S(2)}) async-start(bf16[8,4,128,128]{3,2,1,0:T(8,128)(2,1)} %pack.2), calls=%async_computation | async-start | bytes 2097152 | tf_op jit(solution)/shard_map/all_to_all | solution.py:244
  42.3 18.1 %copy-start = (f32[60]{0:T(128)S(1)}, f32[60]{0:T(128)}, u32[]{:S(2)}) copy-start(f32[60]{0:T(128)} %reshape.27.refs_4_.bias_ref) | copy-start | bytes 724
  42.3 16.3 %collective-permute-start.2 = (bf16[12,128,128]{2,1,0:T(8,128)(2,1)S(1)}, bf16[12,128,128]{2,1,0:T(8,128)(2,1)S(1)}, u32[]{:S(2)}, u32[]{:S(2)}) collective-permute-start(bf16[12,128,128]{2,1,0:T(8,128)(2,1)S(1)} %get-tuple-element.12), channel_id=1, source_target_pairs={{0,8},{8,16},{16,24},{24,32},{32,40},{40,48},{48,56},{56,64},{64,7... | collective-permute-start | bytes 1179656 | tf_op jit(solution)/shard_map/ppermute | solution.py:247
  44.3 16.1 %collective-permute-start.3 = (bf16[12,128,128]{2,1,0:T(8,128)(2,1)S(1)}, bf16[12,128,128]{2,1,0:T(8,128)(2,1)S(1)}, u32[]{:S(2)}, u32[]{:S(2)}) collective-permute-start(bf16[12,128,128]{2,1,0:T(8,128)(2,1)S(1)} %get-tuple-element.13), channel_id=1, source_target_pairs={{8,0},{16,8},{24,16},{32,24},{40,32},{48,40},{56,48},{64,56},{72,6... | collective-permute-start | bytes 1179656 | tf_op jit(solution)/shard_map/ppermute | solution.py:248
  71.4 32.6 %all-to-all-start.3 = ((bf16[8,3,128,128]{3,2,1,0:T(8,128)(2,1)}), bf16[8,3,128,128]{3,2,1,0:T(8,128)(2,1)S(1)}, u32[]{:S(2)}, u32[]{:S(2)}) async-start(bf16[8,3,128,128]{3,2,1,0:T(8,128)(2,1)} %attend.3), calls=%async_computation.3 | async-start | bytes 1572864 | tf_op jit(solution)/shard_map/all_to_all | solution.py:250
  78.2 13.1 %collective-permute-start = (bf16[12,128,128]{2,1,0:T(8,128)(2,1)S(1)}, bf16[12,128,128]{2,1,0:T(8,128)(2,1)S(1)}, u32[]{:S(2)}, u32[]{:S(2)}) collective-permute-start(bf16[12,128,128]{2,1,0:T(8,128)(2,1)S(1)} %get-tuple-element.10), channel_id=1, source_target_pairs={{0,8},{8,16},{16,24},{24,32},{32,40},{40,48},{48,56},{56,64},{64,7... | collective-permute-start | bytes 1179656 | tf_op jit(solution)/shard_map/ppermute | solution.py:247
  80.2 12.9 %collective-permute-start.1 = (bf16[12,128,128]{2,1,0:T(8,128)(2,1)S(1)}, bf16[12,128,128]{2,1,0:T(8,128)(2,1)S(1)}, u32[]{:S(2)}, u32[]{:S(2)}) collective-permute-start(bf16[12,128,128]{2,1,0:T(8,128)(2,1)S(1)} %get-tuple-element.11), channel_id=1, source_target_pairs={{8,0},{16,8},{24,16},{32,24},{40,32},{48,40},{56,48},{64,56},{72,6... | collective-permute-start | bytes 1179656 | tf_op jit(solution)/shard_map/ppermute | solution.py:248
  104.0 26.2 %all-to-all-start.1 = ((bf16[8,3,128,128]{3,2,1,0:T(8,128)(2,1)}), bf16[8,3,128,128]{3,2,1,0:T(8,128)(2,1)S(1)}, u32[]{:S(2)}, u32[]{:S(2)}) async-start(bf16[8,3,128,128]{3,2,1,0:T(8,128)(2,1)} %attend.2), calls=%async_computation.1 | async-start | bytes 1572864 | tf_op jit(solution)/shard_map/all_to_all | solution.py:250
where the time goes:
time: 133 us; the launch traced here: 132 us
  waiting for transfers between devices  52 us (39%)
  starting transfers between devices  46.6 us (35%)
  Pallas kernels  30.7 us (23%)
  local copies, waits for them, and re-layouts  2.03 us (2%)
    all_to_all x2, waiting for transfers between devices, per_device(): lax.all_to_all(packed, 'blk', split_axis=0, concat_axis=0, tiled=True)  24.3 us
    pallas_call x2, Pallas kernels, attend(): pl.pallas_call(attend_body, in_specs=[pl.BlockSpec(memory_space=pltpu.SME...  21.9 us
    ppermute x2, starting transfers between devices, per_device(): right = lax.ppermute(low, 'seq', down)  18.5 us
    all_to_all x2, waiting for transfers between devices, per_device(): back = lax.all_to_all(out, 'blk', split_axis=0, concat_axis=0, tiled=True)  17.2 us
    all_to_all x2, starting transfers between devices, per_device(): back = lax.all_to_all(out, 'blk', split_axis=0, concat_axis=0, tiled=True)  13.6 us
    all_to_all x2, starting transfers between devices, per_device(): lax.all_to_all(packed, 'blk', split_axis=0, concat_axis=0, tiled=True)  10.7 us
    ppermute x2, waiting for transfers between devices, per_device(): left = lax.ppermute(high, 'seq', up)  7.03 us
    pallas_call x2, Pallas kernels, pack(): pl.pallas_call(body, in_specs=[pl.BlockSpec(memory_space=pl.ANY)] * (coun...  4.44 us
  transfers between devices with their start and end apart: 8, of which 7 were waited for; matrix products, arithmetic and copies ran while one was open for 1% of the time, Pallas kernels for 20%

commit v1 on v0

v1 whole, which is shorter than its diff:
```python
import jax
import jax.numpy as jnp
from jax import lax
from jax.experimental import pallas as pl
from jax.experimental.pallas import tpu as pltpu
from jax.sharding import PartitionSpec as P


HEAD_DIM = 64
TILE = 128
REACH = 2
LANES = 128
WINDOW = 2 * REACH + 1
SPAN = WINDOW * TILE
SCALE = float(HEAD_DIM) ** (-0.5)
AXES = ("seq", "blk")
CORES = 2
VMEM = pl.BlockSpec(memory_space=pltpu.VMEM)
NT = (((1,), (1,)), ((), ()))
TN = (((0,), (0,)), ((), ()))


def cost(flops, moved, exps=0):
    return pl.CostEstimate(flops=flops, bytes_accessed=moved, transcendentals=exps)


def pack(arrays, peers):
    rows, count = arrays[0].shape[0], len(arrays)

    def body(*refs):
        ins, refs = refs[:count], refs[count:]
        out_ref, held, in_sem, out_sem = refs
        reads = [
            [
                pltpu.make_async_copy(ins[n].at[:, pl.ds(b * LANES, LANES)], held.at[b, n], in_sem.at[b, n])
                for n in range(count)
            ]
            for b in range(peers)
        ]
        writes = [pltpu.make_async_copy(held.at[b], out_ref.at[b], out_sem.at[b]) for b in range(peers)]
        for b in range(peers):
            for n in range(count):
                reads[b][n].start()
        for b in range(peers):
            for n in range(count):
                reads[b][n].wait()
            writes[b].start()
        for b in range(peers):
            writes[b].wait()

    shape = (peers, count, rows, LANES)
    return pl.pallas_call(
        body,
        in_specs=[pl.BlockSpec(memory_space=pl.ANY)] * count,
        out_specs=pl.BlockSpec(memory_space=pl.ANY),
        out_shape=jax.ShapeDtypeStruct(shape, jnp.bfloat16),
        scratch_shapes=[
            pltpu.VMEM(shape, jnp.bfloat16),
            pltpu.SemaphoreType.DMA((peers, count)),
            pltpu.SemaphoreType.DMA((peers,)),
        ],
        cost_estimate=cost(0, 2 * peers * count * rows * LANES * 2),
        name="pack",
    )(*arrays)


def unpack(grads):
    peers, count, rows, _ = grads.shape

    def body(in_ref, *refs):
        outs, sem = refs[:count], refs[count]
        copies = [
            pltpu.make_async_copy(in_ref.at[b, n], outs[n].at[:, pl.ds(b * LANES, LANES)], sem.at[b, n])
            for b in range(peers)
            for n in range(count)
        ]
        for copy in copies:
            copy.start()
        for copy in copies:
            copy.wait()

    return pl.pallas_call(
        body,
        in_specs=[pl.BlockSpec(memory_space=pl.ANY)],
        out_specs=[pl.BlockSpec(memory_space=pl.ANY)] * count,
        out_shape=[jax.ShapeDtypeStruct((rows, peers * LANES), jnp.bfloat16)] * count,
        scratch_shapes=[pltpu.SemaphoreType.DMA((peers, count))],
        compiler_params=pltpu.CompilerParams(vmem_limit_bytes=4 << 20),
        cost_estimate=cost(0, 2 * peers * count * rows * LANES * 2),
        name="unpack",
    )(grads)


def rim_body(x_ref, after_ref, low_ref, high_ref):
    tiles = x_ref.shape[0]
    deep = 2 * REACH
    for ref, wide, narrow in ((low_ref, 0, 0), (high_ref, tiles - deep, tiles - REACH)):
        for t in range(deep):
            ref[t] = x_ref[wide + t, 1]
            ref[deep + t] = x_ref[wide + t, 2]
        for t in range(REACH):
            ref[2 * deep + t] = x_ref[narrow + t, 0]
            ref[2 * deep + REACH + t] = x_ref[narrow + t, 3]


def rims(taken, after):
    shape = jax.ShapeDtypeStruct((6 * REACH,) + taken.shape[2:], taken.dtype)
    return pl.pallas_call(
        rim_body,
        in_specs=[VMEM, pl.BlockSpec(memory_space=pl.ANY)],
        out_specs=[VMEM] * 2,
        out_shape=[shape] * 2,
        compiler_params=pltpu.CompilerParams(vmem_limit_bytes=8 << 20),
        cost_estimate=cost(0, 2 << 20),
        name="rims",
    )(taken, after)


def both_heads(block):
    first = lax.broadcasted_iota(jnp.int32, block.shape, 1) < HEAD_DIM
    zero = jnp.zeros_like(block)
    return jnp.concatenate([jnp.where(first, block, zero), jnp.where(first, zero, block)], axis=0)


def window_grads(bias_ref, row, query_tile, grad_tile, key, value):
    query = both_heads(query_tile * jnp.bfloat16(SCALE))
    grad = both_heads(grad_tile)
    scores = lax.dot_general(key, query, NT, preferred_element_type=jnp.float32)
    scores = jnp.concatenate(
        [scores[t * TILE:(t + 1) * TILE] + bias_ref[row * WINDOW + t] for t in range(WINDOW)], axis=0)
    top = jnp.max(scores, axis=0, keepdims=True)
    weights = jnp.exp(scores - top)
    probs = weights * (1.0 / jnp.sum(weights, axis=0, keepdims=True))
    probs_b = probs.astype(jnp.bfloat16)
    dprobs = lax.dot_general(value, grad, NT, preferred_element_type=jnp.float32)
    delta = jnp.sum(probs_b.astype(jnp.float32) * dprobs, axis=0, keepdims=True)
    dscores = (probs * (dprobs - delta)).astype(jnp.bfloat16)
    return query, grad, probs_b, dscores


def query_grad(dscores, key):
    both = lax.dot_general(dscores, key, TN, preferred_element_type=jnp.float32)
    first = lax.broadcasted_iota(jnp.int32, (TILE, LANES), 1) < HEAD_DIM
    return (jnp.where(first, both[:TILE], both[TILE:]) * SCALE).astype(jnp.bfloat16)


def inner_body(bias_ref, x_ref, dquery_ref, mid_ref, edge_ref, key_ref, value_ref, dkey_ref, dvalue_ref):
    tiles = x_ref.shape[0]
    deep = 2 * REACH
    for t in range(tiles):
        key_ref[t * TILE:(t + 1) * TILE] = x_ref[t, 1]
        value_ref[t * TILE:(t + 1) * TILE] = x_ref[t, 2]
    dkey_ref[...] = jnp.zeros_like(dkey_ref)
    dvalue_ref[...] = jnp.zeros_like(dvalue_ref)

    def step(n):
        rows = pl.ds(pl.multiple_of(n * TILE, TILE), SPAN)
        key, value = key_ref[rows], value_ref[rows]
        query, grad, probs_b, dscores = window_grads(
            bias_ref, n + 2 * REACH, x_ref[n + REACH, 0], x_ref[n + REACH, 3], key, value)
        dkey_ref[rows] += jnp.dot(dscores, query, preferred_element_type=jnp.float32)
        dvalue_ref[rows] += jnp.dot(probs_b, grad, preferred_element_type=jnp.float32)
        dquery_ref[n] = query_grad(dscores, key)

    def steps(n, _):
        step(2 * n)
        step(2 * n + 1)
        return 0

    lax.fori_loop(0, (tiles - 2 * REACH) // 2, steps, 0)
    for n, ref in ((0, dkey_ref), (1, dvalue_ref)):
        for t in range(tiles):
            block = ref[t * TILE:(t + 1) * TILE]
            if t < deep:
                edge_ref[n, t * TILE:(t + 1) * TILE] = block
            elif t >= tiles - deep:
                at = (t - tiles + 2 * deep) * TILE
                edge_ref[n, at:at + TILE] = block
            else:
                mid_ref[t - deep, n] = block.astype(jnp.bfloat16)


def inner(bias, taken):
    tiles = taken.shape[0]
    steps = tiles - 2 * REACH
    whole = tiles * TILE
    return pl.pallas_call(
        inner_body,
        in_specs=[pl.BlockSpec(memory_space=pltpu.SMEM), VMEM],
        out_specs=[VMEM] * 3,
        out_shape=[
            jax.ShapeDtypeStruct((steps, TILE, LANES), jnp.bfloat16),
            jax.ShapeDtypeStruct((tiles - 4 * REACH, 2, TILE, LANES), jnp.bfloat16),
            jax.ShapeDtypeStruct((2, 4 * REACH * TILE, LANES), jnp.float32),
        ],
        scratch_shapes=[pltpu.VMEM((whole, LANES), jnp.bfloat16)] * 2 + [pltpu.VMEM((whole, LANES), jnp.float32)] * 2,
        compiler_params=pltpu.CompilerParams(vmem_limit_bytes=28 << 20),
        cost_estimate=cost(steps * WINDOW * 10 * TILE * TILE * LANES, 5 << 20, steps * WINDOW * 2 * TILE * TILE),
        name="inner",
    )(bias, taken)


def outer_body(bias_ref, x_ref, low_ref, high_ref, dquery_ref, mid_ref, edge_ref, out_ref, key_ref, value_ref, acc_ref):
    tiles = x_ref.shape[0]
    deep = 2 * REACH
    for n, ref in ((1, key_ref), (2, value_ref)):
        for t in range(deep):
            ref[t * TILE:(t + 1) * TILE] = low_ref[(n - 1) * deep + t]
            ref[(deep + t) * TILE:(deep + t + 1) * TILE] = x_ref[t, n]
            ref[(2 * deep + t) * TILE:(2 * deep + t + 1) * TILE] = x_ref[tiles - deep + t, n]
            ref[(3 * deep + t) * TILE:(3 * deep + t + 1) * TILE] = high_ref[(n - 1) * deep + t]
    acc_ref[...] = edge_ref[...]
    for t in range(tiles - 2 * REACH):
        out_ref[REACH + t, 0] = dquery_ref[t]
    for t in range(tiles - 2 * deep):
        out_ref[deep + t, 1] = mid_ref[t, 0]
        out_ref[deep + t, 2] = mid_ref[t, 1]
    for j in range(deep):
        for high in (False, True):
            start = j + (2 * deep if high else 0)
            rows = slice(start * TILE, (start + WINDOW) * TILE)
            key, value = key_ref[rows], value_ref[rows]
            own = (j < REACH) == high
            tile = (tiles - REACH + j if high else j - REACH) if own else None
            row = j + tiles if high else j
            if own:
                query_tile, grad_tile = x_ref[tile, 0], x_ref[tile, 3]
            else:
                ref, at = (high_ref, j - REACH) if high else (low_ref, j)
                query_tile, grad_tile = ref[2 * deep + at], ref[2 * deep + REACH + at]
            query, grad, probs_b, dscores = window_grads(bias_ref, row, query_tile, grad_tile, key, value)
            if high:
                first, last = max(start, 2 * deep), min(start + WINDOW, 3 * deep)
            else:
                first, last = max(start, deep), min(start + WINDOW, 2 * deep)
            part = slice((first - start) * TILE, (last - start) * TILE)
            at = slice((first - deep) * TILE, (last - deep) * TILE)
            acc_ref[0, at] += jnp.dot(dscores[part], query, preferred_element_type=jnp.float32)
            acc_ref[1, at] += jnp.dot(probs_b[part], grad, preferred_element_type=jnp.float32)
            if own:
                out_ref[tile, 0] = query_grad(dscores, key)
    for n in range(2):
        for t in range(2 * deep):
            tile = t if t < deep else tiles - 2 * deep + t
            out_ref[tile, 1 + n] = acc_ref[n, t * TILE:(t + 1) * TILE].astype(jnp.bfloat16)


def outer(bias, taken, low, high, dquery, mid, edge):
    tiles = taken.shape[0]
    steps = 4 * REACH
    return pl.pallas_call(
        outer_body,
        in_specs=[pl.BlockSpec(memory_space=pltpu.SMEM)] + [VMEM] * 6,
        out_specs=VMEM,
        out_shape=jax.ShapeDtypeStruct((tiles, 3, TILE, LANES), jnp.bfloat16),
        scratch_shapes=[pltpu.VMEM((8 * REACH * TILE, LANES), jnp.bfloat16)] * 2
        + [pltpu.VMEM(edge.shape, jnp.float32)],
        compiler_params=pltpu.CompilerParams(vmem_limit_bytes=28 << 20),
        cost_estimate=cost(steps * WINDOW * 8 * TILE * TILE * LANES, 6 << 20, steps * WINDOW * 2 * TILE * TILE),
        name="outer",
    )(bias, taken, low, high, dquery, mid, edge)


def tile_bias(near_mask, motion_count, first, tiles):
    total = near_mask.shape[0]
    near = lax.dynamic_slice_in_dim(jnp.pad(near_mask, ((REACH, REACH), (0, 0))), first, tiles + 2 * REACH, 0) == 1
    far = lax.dynamic_slice_in_dim(jnp.pad(motion_count, (REACH, REACH)), first, tiles + 2 * REACH, 0) >= 2
    own = jnp.ones_like(far)
    allowed = jnp.stack([far, near[:, 0], own, near[:, 1], far], axis=1)
    index = first - REACH + jnp.arange(tiles + 2 * REACH)
    others = index[:, None] + jnp.arange(-REACH, REACH + 1)[None, :]
    allowed &= (others >= 0) & (others < total)
    return jnp.where(allowed, 0.0, -1e30).astype(jnp.float32).reshape(-1)


def per_device(query_states, key_states, value_states, output_grad, near_mask, motion_count):
    blocks, spans = lax.axis_size("blk"), lax.axis_size("seq")
    tiles = CORES * blocks
    groups = [[g * tiles + t for t in range(tiles)] for g in range(spans // CORES)]

    def exchange(x):
        return lax.all_to_all(x, AXES, split_axis=0, concat_axis=0, tiled=True, axis_index_groups=groups)

    up = [(i, i + CORES) for i in range(spans - CORES)]
    down = [(j, i) for i, j in up]
    bias = tile_bias(near_mask, motion_count, lax.axis_index("seq") // CORES * tiles, tiles)
    packed = pack((query_states, key_states, value_states, output_grad), tiles)
    taken = exchange(packed)
    first, last = rims(taken, bias)
    low = lax.ppermute(last, "seq", up)
    high = lax.ppermute(first, "seq", down)
    parts = inner(bias, taken)
    out = outer(bias, taken, low, high, *parts)
    back = exchange(out)
    return tuple(unpack(back))


def solution(mesh):
    spec = P(AXES, None)
    return jax.shard_map(
        per_device, mesh=mesh, in_specs=(spec,) * 4 + (P(), P()), out_specs=(spec,) * 3, check_vma=False
    )
```

time: 133 us -> 136 us (1.023)
  the two profiles are of different devices: /device:TPU:6 before, /device:TPU:7 now
where the time goes in v1:
time: 136 us; the launch traced here: 134 us
  waiting for transfers between devices  47.2 us (35%)
  blocking collectives  43.5 us (32%)
  Pallas kernels  21.8 us (16%)
  starting transfers between devices  20.7 us (15%)
    all_to_all x1, waiting for transfers between devices, exchange(): lax.all_to_all(x, AXES, split_axis=0, concat_axis=0, tiled=True, axis_ind...  47.2 us
    all_to_all x1, blocking collectives, exchange(): lax.all_to_all(x, AXES, split_axis=0, concat_axis=0, tiled=True, axis_ind...  43.5 us
    pallas_call x1, Pallas kernels, inner(): pl.pallas_call(inner_body, in_specs=[pl.BlockSpec(memory_space=pltpu.SMEM...  11 us
    ppermute x1, starting transfers between devices, per_device(): high = lax.ppermute(first, 'seq', down)  8.85 us
    all_to_all x1, starting transfers between devices, exchange(): lax.all_to_all(x, AXES, split_axis=0, concat_axis=0, tiled=True, axis_ind...  7.8 us
    pallas_call x1, Pallas kernels, outer(): pl.pallas_call(outer_body, in_specs=[pl.BlockSpec(memory_space=pltpu.SMEM...  6.22 us
    ppermute x1, starting transfers between devices, per_device(): low = lax.ppermute(last, 'seq', up)  4 us
    pallas_call x1, Pallas kernels, pack(): pl.pallas_call(body, in_specs=[pl.BlockSpec(memory_space=pl.ANY)] * count...  2.97 us
  transfers between devices with their start and end apart: 3, of which 1 were waited for; matrix products, arithmetic and copies ran while one was open for 0% of the time, Pallas kernels for 8%

profile of v1, /device:TPU:7, one launch (start us, length us, event | category | flops | bytes accessed | tf_op | source)
XLA Modules:
  0.0 134.4 jit_solution(17721092496165630280)
XLA Ops:
  0.6 3.0 %pack.1 = bf16[16,4,128,128]{3,2,1,0:T(8,128)(2,1)} custom-call(bf16[128,2048]{1,0:T(8,128)(2,1)} %refs_0_.1, bf16[128,2048]{1,0:T(8,128)(2,1)} %refs_1_.1, bf16[128,2048]{1,0:T(8,128)(2,1)} %refs_2_.1, bf16[128,2048]{1,0:T(8,128)(2,1)} %refs_3_.1), custom_call_target="tpu_custom_call" | custom-call | bytes 4194304 | tf_op jit(solution)/shard_map/pack/pallas_call | solution.py:52
  3.6 0.0 copy-start
  3.6 0.0 copy-start.1
  3.6 7.8 %all-to-all-start = ((bf16[16,4,128,128]{3,2,1,0:T(8,128)(2,1)}), bf16[16,4,128,128]{3,2,1,0:T(8,128)(2,1)S(1)}, u32[]{:S(2)}, u32[]{:S(2)}) async-start(bf16[16,4,128,128]{3,2,1,0:T(8,128)(2,1)} %pack.1), calls=%async_computation | async-start | bytes 4194304 | tf_op jit(solution)/shard_map/all_to_all | solution.py:282
  11.4 0.0 copy-done
  11.4 0.1 fusion.3
  11.5 0.0 copy-done.1
  11.5 0.1 compare_bitcast_fusion
  11.7 0.1 fusion.2
  11.8 0.1 copy.10
  11.9 0.1 reshape.27.after_ref.bias_ref
  11.9 47.2 %all-to-all-done.x_ref = bf16[16,4,128,128]{3,2,1,0:T(8,128)(2,1)S(1)} async-done(((bf16[16,4,128,128]{3,2,1,0:T(8,128)(2,1)}), bf16[16,4,128,128]{3,2,1,0:T(8,128)(2,1)S(1)}, u32[]{:S(2)}, u32[]{:S(2)}) %all-to-all-start) | async-done | bytes 2097184 | tf_op jit(solution)/shard_map/all_to_all | solution.py:282
  59.2 0.1 rims.1
  59.2 4.0 %collective-permute-start = (bf16[12,128,128]{2,1,0:T(8,128)(2,1)S(1)}, bf16[12,128,128]{2,1,0:T(8,128)(2,1)S(1)}, u32[]{:S(2)}, u32[]{:S(2)}) collective-permute-start(bf16[12,128,128]{2,1,0:T(8,128)(2,1)S(1)} %get-tuple-element.8), channel_id=1, source_target_pairs={{0,16},{8,24},{16,32},{24,40},{32,48},{40,56},{48,64},{56,72},{64,... | collective-permute-start | bytes 1179656 | tf_op jit(solution)/shard_map/ppermute | solution.py:290
  63.2 8.9 %collective-permute-start.1 = (bf16[12,128,128]{2,1,0:T(8,128)(2,1)S(1)}, bf16[12,128,128]{2,1,0:T(8,128)(2,1)S(1)}, u32[]{:S(2)}, u32[]{:S(2)}) collective-permute-start(bf16[12,128,128]{2,1,0:T(8,128)(2,1)S(1)} %get-tuple-element.9), channel_id=1, source_target_pairs={{16,0},{24,8},{32,16},{40,24},{48,32},{56,40},{64,48},{72,56},{80,... | collective-permute-start | bytes 1179656 | tf_op jit(solution)/shard_map/ppermute | solution.py:291
  72.1 11.0 %inner.1 = (bf16[12,128,128]{2,1,0:T(8,128)(2,1)S(1)}, bf16[8,2,128,128]{3,2,1,0:T(8,128)(2,1)S(1)}, f32[2,1024,128]{2,1,0:T(8,128)S(1)}) custom-call(f32[100]{0:T(128)S(1)} %reshape.27.after_ref.bias_ref, bf16[16,4,128,128]{3,2,1,0:T(8,128)(2,1)S(1)} %all-to-all-done.x_ref), custom_call_target="tpu_custom_call" | custom-call | flops 1258291200 | bytes 5242880 | tf_op jit(solution)/shard_map/inner/pallas_call | solution.py:187
  83.1 0.0 collective-permute-done.low_ref
  83.1 0.0 collective-permute-done.1.high_ref
  83.1 6.2 %outer.1 = bf16[16,3,128,128]{3,2,1,0:T(8,128)(2,1)S(1)} custom-call(f32[100]{0:T(128)S(1)} %reshape.27.after_ref.bias_ref, bf16[16,4,128,128]{3,2,1,0:T(8,128)(2,1)S(1)} %all-to-all-done.x_ref, bf16[12,128,128]{2,1,0:T(8,128)(2,1)S(1)} %collective-permute-done.low_ref, bf16[12,128,128]{2,1,0:T(8,128)(2,1)S(1)} %collective-permute-done.1.high_ref, ...), custom_call_target="tpu_custom_call" | custom-call | flops 671088640 | bytes 6291456 | tf_op jit(solution)/shard_map/outer/pallas_call | solution.py:251
  89.3 43.5 %all_to_all.10.in_ref = bf16[16,3,128,128]{3,2,1,0:T(8,128)(2,1)S(1)} all-to-all(bf16[16,3,128,128]{3,2,1,0:T(8,128)(2,1)S(1)} %outer.1), channel_id=1, replica_groups={{0,1,2,3,4,5,6,7,8,9,10,11,12,13,14,15},{16,17,18,19,20,21,22,23,24,25,..., dimensions={0} | all-to-all | bytes 3145728 | tf_op jit(solution)/shard_map/all_to_all | solution.py:282
  132.8 1.5 %unpack.1 = (bf16[128,2048]{1,0:T(8,128)(2,1)}, bf16[128,2048]{1,0:T(8,128)(2,1)}, bf16[128,2048]{1,0:T(8,128)(2,1)}) custom-call(bf16[16,3,128,128]{3,2,1,0:T(8,128)(2,1)S(1)} %all_to_all.10.in_ref), custom_call_target="tpu_custom_call" | custom-call | bytes 3145728 | tf_op jit(solution)/shard_map/unpack/pallas_call | solution.py:82
  (5 shorter events, 0.1 us)
Async XLA Ops:
  3.6 7.8 %copy-start = (s32[512,2]{0,1:T(2,128)S(1)}, s32[512,2]{0,1:T(2,128)}, u32[]{:S(2)}) copy-start(s32[512,2]{0,1:T(2,128)} %param.10) | copy-start | bytes 12292
  3.6 7.9 %copy-start.1 = (s32[512]{0:T(512)S(1)}, s32[512]{0:T(512)}, u32[]{:S(2)}) copy-start(s32[512]{0:T(512)} %param.11) | copy-start | bytes 6148
  3.6 55.5 %all-to-all-start = ((bf16[16,4,128,128]{3,2,1,0:T(8,128)(2,1)}), bf16[16,4,128,128]{3,2,1,0:T(8,128)(2,1)S(1)}, u32[]{:S(2)}, u32[]{:S(2)}) async-start(bf16[16,4,128,128]{3,2,1,0:T(8,128)(2,1)} %pack.1), calls=%async_computation | async-start | bytes 4194304 | tf_op jit(solution)/shard_map/all_to_all | solution.py:282
  59.2 23.9 %collective-permute-start = (bf16[12,128,128]{2,1,0:T(8,128)(2,1)S(1)}, bf16[12,128,128]{2,1,0:T(8,128)(2,1)S(1)}, u32[]{:S(2)}, u32[]{:S(2)}) collective-permute-start(bf16[12,128,128]{2,1,0:T(8,128)(2,1)S(1)} %get-tuple-element.8), channel_id=1, source_target_pairs={{0,16},{8,24},{16,32},{24,40},{32,48},{40,56},{48,64},{56,72},{64,... | collective-permute-start | bytes 1179656 | tf_op jit(solution)/shard_map/ppermute | solution.py:290
  63.2 19.9 %collective-permute-start.1 = (bf16[12,128,128]{2,1,0:T(8,128)(2,1)S(1)}, bf16[12,128,128]{2,1,0:T(8,128)(2,1)S(1)}, u32[]{:S(2)}, u32[]{:S(2)}) collective-permute-start(bf16[12,128,128]{2,1,0:T(8,128)(2,1)S(1)} %get-tuple-element.9), channel_id=1, source_target_pairs={{16,0},{24,8},{32,16},{40,24},{48,32},{56,40},{64,48},{72,56},{80,... | collective-permute-start | bytes 1179656 | tf_op jit(solution)/shard_map/ppermute | solution.py:291

commit v2 on v1

--- a/solution.py
+++ b/solution.py
@@ -91,10 +91,13 @@
     )(grads)
 
 
-def rim_body(x_ref, after_ref, low_ref, high_ref):
+def rim_body(info_ref, x_ref, first_ref, second_ref):
     tiles = x_ref.shape[0]
     deep = 2 * REACH
-    for ref, wide, narrow in ((low_ref, 0, 0), (high_ref, tiles - deep, tiles - REACH)):
+    odd = info_ref[info_ref.shape[0] - 1] > 0.5
+    for ref, low in ((first_ref, odd), (second_ref, jnp.logical_not(odd))):
+        wide = jnp.where(low, 0, tiles - deep)
+        narrow = jnp.where(low, 0, tiles - REACH)
         for t in range(deep):
             ref[t] = x_ref[wide + t, 1]
             ref[deep + t] = x_ref[wide + t, 2]
@@ -103,17 +106,17 @@
             ref[2 * deep + REACH + t] = x_ref[narrow + t, 3]
 
 
-def rims(taken, after):
+def rims(info, taken):
     shape = jax.ShapeDtypeStruct((6 * REACH,) + taken.shape[2:], taken.dtype)
     return pl.pallas_call(
         rim_body,
-        in_specs=[VMEM, pl.BlockSpec(memory_space=pl.ANY)],
+        in_specs=[pl.BlockSpec(memory_space=pltpu.SMEM), VMEM],
         out_specs=[VMEM] * 2,
         out_shape=[shape] * 2,
         compiler_params=pltpu.CompilerParams(vmem_limit_bytes=8 << 20),
         cost_estimate=cost(0, 2 << 20),
         name="rims",
-    )(taken, after)
+    )(info, taken)
 
 
 def both_heads(block):
@@ -122,20 +125,41 @@
     return jnp.concatenate([jnp.where(first, block, zero), jnp.where(first, zero, block)], axis=0)
 
 
-def window_grads(bias_ref, row, query_tile, grad_tile, key, value):
+def score_stage(bias_ref, row, query_tile, grad_tile, key, value, held):
+    scores_ref, dprobs_ref, query_ref, grad_ref = held[:4]
     query = both_heads(query_tile * jnp.bfloat16(SCALE))
     grad = both_heads(grad_tile)
     scores = lax.dot_general(key, query, NT, preferred_element_type=jnp.float32)
-    scores = jnp.concatenate(
-        [scores[t * TILE:(t + 1) * TILE] + bias_ref[row * WINDOW + t] for t in range(WINDOW)], axis=0)
-    top = jnp.max(scores, axis=0, keepdims=True)
-    weights = jnp.exp(scores - top)
-    probs = weights * (1.0 / jnp.sum(weights, axis=0, keepdims=True))
-    probs_b = probs.astype(jnp.bfloat16)
-    dprobs = lax.dot_general(value, grad, NT, preferred_element_type=jnp.float32)
-    delta = jnp.sum(probs_b.astype(jnp.float32) * dprobs, axis=0, keepdims=True)
-    dscores = (probs * (dprobs - delta)).astype(jnp.bfloat16)
-    return query, grad, probs_b, dscores
+    for t in range(WINDOW):
+        rows = slice(t * TILE, (t + 1) * TILE)
+        scores_ref[rows] = scores[rows] + bias_ref[row * WINDOW + t]
+    dprobs_ref[...] = lax.dot_general(value, grad, NT, preferred_element_type=jnp.float32)
+    query_ref[...] = query
+    grad_ref[...] = grad
+
+
+def softmax_stage(held):
+    scores_ref, dprobs_ref, _, _, probs_ref, dscores_ref = held
+    parts = [slice(t * TILE, (t + 1) * TILE) for t in range(WINDOW)]
+    top = jnp.max(scores_ref[...], axis=0, keepdims=True)
+    total = jnp.zeros_like(top)
+    for rows in parts:
+        weights = jnp.exp(scores_ref[rows] - top)
+        scores_ref[rows] = weights
+        total += jnp.sum(weights, axis=0, keepdims=True)
+    inverse = 1.0 / total
+    delta = jnp.zeros_like(top)
+    for rows in parts:
+        probs = (scores_ref[rows] * inverse).astype(jnp.bfloat16)
+        probs_ref[rows] = probs
+        delta += jnp.sum(probs.astype(jnp.float32) * dprobs_ref[rows], axis=0, keepdims=True)
+    for rows in parts:
+        dscores_ref[rows] = (scores_ref[rows] * inverse * (dprobs_ref[rows] - delta)).astype(jnp.bfloat16)
+
+
+def held_shapes():
+    wide, tall = (SPAN, 2 * TILE), (2 * TILE, LANES)
+    return [pltpu.VMEM(wide, jnp.float32)] * 2 + [pltpu.VMEM(tall, jnp.bfloat16)] * 2 + [pltpu.VMEM(wide, jnp.bfloat16)] * 2
 
 
 def query_grad(dscores, key):
@@ -144,30 +168,51 @@
     return (jnp.where(first, both[:TILE], both[TILE:]) * SCALE).astype(jnp.bfloat16)
 
 
-def inner_body(bias_ref, x_ref, dquery_ref, mid_ref, edge_ref, key_ref, value_ref, dkey_ref, dvalue_ref):
+def inner_body(bias_ref, x_ref, dquery_ref, mid_ref, edge_ref, key_ref, value_ref, dkey_ref, dvalue_ref, *held):
     tiles = x_ref.shape[0]
     deep = 2 * REACH
+    held = (held[:6], held[6:])
     for t in range(tiles):
         key_ref[t * TILE:(t + 1) * TILE] = x_ref[t, 1]
         value_ref[t * TILE:(t + 1) * TILE] = x_ref[t, 2]
     dkey_ref[...] = jnp.zeros_like(dkey_ref)
     dvalue_ref[...] = jnp.zeros_like(dvalue_ref)
 
-    def step(n):
-        rows = pl.ds(pl.multiple_of(n * TILE, TILE), SPAN)
-        key, value = key_ref[rows], value_ref[rows]
-        query, grad, probs_b, dscores = window_grads(
-            bias_ref, n + 2 * REACH, x_ref[n + REACH, 0], x_ref[n + REACH, 3], key, value)
-        dkey_ref[rows] += jnp.dot(dscores, query, preferred_element_type=jnp.float32)
-        dvalue_ref[rows] += jnp.dot(probs_b, grad, preferred_element_type=jnp.float32)
-        dquery_ref[n] = query_grad(dscores, key)
-
-    def steps(n, _):
-        step(2 * n)
-        step(2 * n + 1)
+    def rows_of(n):
+        return pl.ds(n * TILE if isinstance(n, int) else pl.multiple_of(n * TILE, TILE), SPAN)
+
+    def begin(n, slot):
+        rows = rows_of(n)
+        score_stage(
+            bias_ref, n + 2 * REACH, x_ref[n + REACH, 0], x_ref[n + REACH, 3], key_ref[rows], value_ref[rows], held[slot])
+
+    def end(n, slot):
+        _, _, query_ref, grad_ref, probs_ref, dscores_ref = held[slot]
+        rows = rows_of(n)
+        dscores = dscores_ref[...]
+        dkey_ref[rows] += jnp.dot(dscores, query_ref[...], preferred_element_type=jnp.float32)
+        dvalue_ref[rows] += jnp.dot(probs_ref[...], grad_ref[...], preferred_element_type=jnp.float32)
+        dquery_ref[n] = query_grad(dscores, key_ref[rows])
+
+    steps = tiles - 2 * REACH
+    begin(0, 0)
+    softmax_stage(held[0])
+    begin(1, 1)
+
+    def pair(k, _):
+        n = 2 * k
+        end(n, 0)
+        softmax_stage(held[1])
+        begin(n + 2, 0)
+        end(n + 1, 1)
+        softmax_stage(held[0])
+        begin(n + 3, 1)
         return 0
 
-    lax.fori_loop(0, (tiles - 2 * REACH) // 2, steps, 0)
+    lax.fori_loop(0, steps // 2 - 1, pair, 0)
+    end(steps - 2, 0)
+    softmax_stage(held[1])
+    end(steps - 1, 1)
     for n, ref in ((0, dkey_ref), (1, dvalue_ref)):
         for t in range(tiles):
             block = ref[t * TILE:(t + 1) * TILE]
@@ -193,16 +238,24 @@
             jax.ShapeDtypeStruct((tiles - 4 * REACH, 2, TILE, LANES), jnp.bfloat16),
             jax.ShapeDtypeStruct((2, 4 * REACH * TILE, LANES), jnp.float32),
         ],
-        scratch_shapes=[pltpu.VMEM((whole, LANES), jnp.bfloat16)] * 2 + [pltpu.VMEM((whole, LANES), jnp.float32)] * 2,
+        scratch_shapes=[pltpu.VMEM((whole, LANES), jnp.bfloat16)] * 2 + [pltpu.VMEM((whole, LANES), jnp.float32)] * 2
+        + held_shapes() * 2,
         compiler_params=pltpu.CompilerParams(vmem_limit_bytes=28 << 20),
         cost_estimate=cost(steps * WINDOW * 10 * TILE * TILE * LANES, 5 << 20, steps * WINDOW * 2 * TILE * TILE),
         name="inner",
     )(bias, taken)
 
 
-def outer_body(bias_ref, x_ref, low_ref, high_ref, dquery_ref, mid_ref, edge_ref, out_ref, key_ref, value_ref, acc_ref):
+def outer_body(
+    bias_ref, x_ref, first_ref, second_ref, dquery_ref, mid_ref, edge_ref, out_ref, halo_ref, key_ref, value_ref, acc_ref, *held
+):
     tiles = x_ref.shape[0]
     deep = 2 * REACH
+    held = (held[:6], held[6:])
+    odd = bias_ref[bias_ref.shape[0] - 1] > 0.5
+    halo_ref[jnp.where(odd, 0, 1)] = first_ref[...]
+    halo_ref[jnp.where(odd, 1, 0)] = second_ref[...]
+    low_ref, high_ref = halo_ref.at[0], halo_ref.at[1]
     for n, ref in ((1, key_ref), (2, value_ref)):
         for t in range(deep):
             ref[t * TILE:(t + 1) * TILE] = low_ref[(n - 1) * deep + t]
@@ -215,37 +268,52 @@
     for t in range(tiles - 2 * deep):
         out_ref[deep + t, 1] = mid_ref[t, 0]
         out_ref[deep + t, 2] = mid_ref[t, 1]
-    for j in range(deep):
-        for high in (False, True):
-            start = j + (2 * deep if high else 0)
-            rows = slice(start * TILE, (start + WINDOW) * TILE)
-            key, value = key_ref[rows], value_ref[rows]
-            own = (j < REACH) == high
-            tile = (tiles - REACH + j if high else j - REACH) if own else None
-            row = j + tiles if high else j
-            if own:
-                query_tile, grad_tile = x_ref[tile, 0], x_ref[tile, 3]
-            else:
-                ref, at = (high_ref, j - REACH) if high else (low_ref, j)
-                query_tile, grad_tile = ref[2 * deep + at], ref[2 * deep + REACH + at]
-            query, grad, probs_b, dscores = window_grads(bias_ref, row, query_tile, grad_tile, key, value)
-            if high:
-                first, last = max(start, 2 * deep), min(start + WINDOW, 3 * deep)
-            else:
-                first, last = max(start, deep), min(start + WINDOW, 2 * deep)
-            part = slice((first - start) * TILE, (last - start) * TILE)
-            at = slice((first - deep) * TILE, (last - deep) * TILE)
-            acc_ref[0, at] += jnp.dot(dscores[part], query, preferred_element_type=jnp.float32)
-            acc_ref[1, at] += jnp.dot(probs_b[part], grad, preferred_element_type=jnp.float32)
-            if own:
-                out_ref[tile, 0] = query_grad(dscores, key)
+
+    def place(step):
+        j, high = step // 2, step % 2 == 1
+        start = j + (2 * deep if high else 0)
+        own = (j < REACH) == high
+        tile = (tiles - REACH + j if high else j - REACH) if own else None
+        return j, high, start, tile
+
+    def begin(step):
+        j, high, start, tile = place(step)
+        rows = slice(start * TILE, (start + WINDOW) * TILE)
+        if tile is not None:
+            query_tile, grad_tile = x_ref[tile, 0], x_ref[tile, 3]
+        else:
+            ref, at = (high_ref, j - REACH) if high else (low_ref, j)
+            query_tile, grad_tile = ref[2 * deep + at], ref[2 * deep + REACH + at]
+        score_stage(
+            bias_ref, j + tiles if high else j, query_tile, grad_tile, key_ref[rows], value_ref[rows], held[step % 2])
+
+    def end(step):
+        _, high, start, tile = place(step)
+        _, _, query_ref, grad_ref, probs_ref, dscores_ref = held[step % 2]
+        low_end, high_end = (2 * deep, 3 * deep) if high else (deep, 2 * deep)
+        first, last = max(start, low_end), min(start + WINDOW, high_end)
+        part = slice((first - start) * TILE, (last - start) * TILE)
+        at = slice((first - deep) * TILE, (last - deep) * TILE)
+        acc_ref[0, at] += jnp.dot(dscores_ref[part], query_ref[...], preferred_element_type=jnp.float32)
+        acc_ref[1, at] += jnp.dot(probs_ref[part], grad_ref[...], preferred_element_type=jnp.float32)
+        if tile is not None:
+            out_ref[tile, 0] = query_grad(dscores_ref[...], key_ref[start * TILE:(start + WINDOW) * TILE])
+
+    steps = 2 * deep
+    for step in range(steps + 2):
+        if step >= 2:
+            end(step - 2)
+        if 1 <= step <= steps:
+            softmax_stage(held[(step - 1) % 2])
+        if step < steps:
+            begin(step)
     for n in range(2):
         for t in range(2 * deep):
             tile = t if t < deep else tiles - 2 * deep + t
             out_ref[tile, 1 + n] = acc_ref[n, t * TILE:(t + 1) * TILE].astype(jnp.bfloat16)
 
 
-def outer(bias, taken, low, high, dquery, mid, edge):
+def outer(bias, taken, first, second, dquery, mid, edge):
     tiles = taken.shape[0]
     steps = 4 * REACH
     return pl.pallas_call(
@@ -253,12 +321,14 @@
         in_specs=[pl.BlockSpec(memory_space=pltpu.SMEM)] + [VMEM] * 6,
         out_specs=VMEM,
         out_shape=jax.ShapeDtypeStruct((tiles, 3, TILE, LANES), jnp.bfloat16),
-        scratch_shapes=[pltpu.VMEM((8 * REACH * TILE, LANES), jnp.bfloat16)] * 2
-        + [pltpu.VMEM(edge.shape, jnp.float32)],
+        scratch_shapes=[pltpu.VMEM((2,) + first.shape, jnp.bfloat16)]
+        + [pltpu.VMEM((8 * REACH * TILE, LANES), jnp.bfloat16)] * 2
+        + [pltpu.VMEM(edge.shape, jnp.float32)]
+        + held_shapes() * 2,
         compiler_params=pltpu.CompilerParams(vmem_limit_bytes=28 << 20),
         cost_estimate=cost(steps * WINDOW * 8 * TILE * TILE * LANES, 6 << 20, steps * WINDOW * 2 * TILE * TILE),
         name="outer",
-    )(bias, taken, low, high, dquery, mid, edge)
+    )(bias, taken, first, second, dquery, mid, edge)
 
 
 def tile_bias(near_mask, motion_count, first, tiles):
@@ -270,7 +340,8 @@
     index = first - REACH + jnp.arange(tiles + 2 * REACH)
     others = index[:, None] + jnp.arange(-REACH, REACH + 1)[None, :]
     allowed &= (others >= 0) & (others < total)
-    return jnp.where(allowed, 0.0, -1e30).astype(jnp.float32).reshape(-1)
+    odd = (first // tiles % 2).astype(jnp.float32)
+    return jnp.concatenate([jnp.where(allowed, 0.0, -1e30).astype(jnp.float32).reshape(-1), odd[None]])
 
 
 def per_device(query_states, key_states, value_states, output_grad, near_mask, motion_count):
@@ -281,16 +352,18 @@
     def exchange(x):
         return lax.all_to_all(x, AXES, split_axis=0, concat_axis=0, tiled=True, axis_index_groups=groups)
 
-    up = [(i, i + CORES) for i in range(spans - CORES)]
-    down = [(j, i) for i, j in up]
+    def swap(x, parity):
+        right = [(i, i + CORES) for i in range(spans - CORES) if i // CORES % 2 == parity]
+        return lax.ppermute(x, "seq", right + [(j, i) for i, j in right])
+
     bias = tile_bias(near_mask, motion_count, lax.axis_index("seq") // CORES * tiles, tiles)
     packed = pack((query_states, key_states, value_states, output_grad), tiles)
     taken = exchange(packed)
-    first, last = rims(taken, bias)
-    low = lax.ppermute(last, "seq", up)
-    high = lax.ppermute(first, "seq", down)
+    first, second = rims(bias, taken)
+    first = swap(first, 0)
+    second = swap(second, 1)
     parts = inner(bias, taken)
-    out = outer(bias, taken, low, high, *parts)
+    out = outer(bias, taken, first, second, *parts)
     back = exchange(out)
     return tuple(unpack(back))
 

time: 136 us -> 135 us (level)
  Pallas kernels: 21.8 us -> 20.1 us
where the time goes in v2:
time: 135 us; the launch traced here: 133 us
  waiting for transfers between devices  47.1 us (35%)
  blocking collectives  43.8 us (32%)
  starting transfers between devices  20.9 us (15%)
  Pallas kernels  20.1 us (15%)
    all_to_all x1, waiting for transfers between devices, exchange(): lax.all_to_all(x, AXES, split_axis=0, concat_axis=0, tiled=True, axis_ind...  47.1 us
    all_to_all x1, blocking collectives, exchange(): lax.all_to_all(x, AXES, split_axis=0, concat_axis=0, tiled=True, axis_ind...  43.8 us
    ppermute x2, starting transfers between devices, swap(): return lax.ppermute(x, 'seq', right + [(j, i) for i, j in right])  13.1 us
    pallas_call x1, Pallas kernels, inner(): pl.pallas_call(inner_body, in_specs=[pl.BlockSpec(memory_space=pltpu.SMEM...  10.1 us
    all_to_all x1, starting transfers between devices, exchange(): lax.all_to_all(x, AXES, split_axis=0, concat_axis=0, tiled=True, axis_ind...  7.8 us
    pallas_call x1, Pallas kernels, outer(): pl.pallas_call(outer_body, in_specs=[pl.BlockSpec(memory_space=pltpu.SMEM...  4.87 us
    pallas_call x1, Pallas kernels, pack(): pl.pallas_call(body, in_specs=[pl.BlockSpec(memory_space=pl.ANY)] * count...  2.97 us
  transfers between devices with their start and end apart: 3, of which 1 were waited for; matrix products, arithmetic and copies ran while one was open for 0% of the time, Pallas kernels for 8%

profile of v2, /device:TPU:7, one launch (start us, length us, event | category | flops | bytes accessed | tf_op | source)
XLA Modules:
  0.0 133.2 jit_solution(13553717745812790152)
XLA Ops:
  0.6 3.0 %pack.1 = bf16[16,4,128,128]{3,2,1,0:T(8,128)(2,1)} custom-call(bf16[128,2048]{1,0:T(8,128)(2,1)} %refs_0_.1, bf16[128,2048]{1,0:T(8,128)(2,1)} %refs_1_.1, bf16[128,2048]{1,0:T(8,128)(2,1)} %refs_2_.1, bf16[128,2048]{1,0:T(8,128)(2,1)} %refs_3_.1), custom_call_target="tpu_custom_call" | custom-call | bytes 4194304 | tf_op jit(solution)/shard_map/pack/pallas_call | solution.py:52
  3.6 0.0 copy-start
  3.6 0.0 copy-start.1
  3.6 7.8 %all-to-all-start = ((bf16[16,4,128,128]{3,2,1,0:T(8,128)(2,1)}), bf16[16,4,128,128]{3,2,1,0:T(8,128)(2,1)S(1)}, u32[]{:S(2)}, u32[]{:S(2)}) async-start(bf16[16,4,128,128]{3,2,1,0:T(8,128)(2,1)} %pack.1), calls=%async_computation | async-start | bytes 4194304 | tf_op jit(solution)/shard_map/all_to_all | solution.py:353
  11.4 0.0 copy-done
  11.4 0.1 fusion.3
  11.5 0.0 copy-done.1
  11.5 0.1 compare_bitcast_fusion
  11.7 0.1 fusion.2
  11.8 0.1 copy.10
  11.9 0.1 reshape.27
  11.9 0.1 pad_maximum_fusion.info_ref.bias_ref
  12.0 47.1 %all-to-all-done.x_ref = bf16[16,4,128,128]{3,2,1,0:T(8,128)(2,1)S(1)} async-done(((bf16[16,4,128,128]{3,2,1,0:T(8,128)(2,1)}), bf16[16,4,128,128]{3,2,1,0:T(8,128)(2,1)S(1)}, u32[]{:S(2)}, u32[]{:S(2)}) %all-to-all-start) | async-done | bytes 2097184 | tf_op jit(solution)/shard_map/all_to_all | solution.py:353
  59.2 0.6 rims.1
  59.8 4.0 %collective-permute-start = (bf16[12,128,128]{2,1,0:T(8,128)(2,1)S(1)}, bf16[12,128,128]{2,1,0:T(8,128)(2,1)S(1)}, u32[]{:S(2)}, u32[]{:S(2)}) collective-permute-start(bf16[12,128,128]{2,1,0:T(8,128)(2,1)S(1)} %get-tuple-element.8), channel_id=1, source_target_pairs={{0,16},{8,24},{32,48},{40,56},{64,80},{72,88},{96,112},{104,120},{... | collective-permute-start | bytes 1179656 | tf_op jit(solution)/shard_map/ppermute | solution.py:357
  63.8 9.1 %collective-permute-start.1 = (bf16[12,128,128]{2,1,0:T(8,128)(2,1)S(1)}, bf16[12,128,128]{2,1,0:T(8,128)(2,1)S(1)}, u32[]{:S(2)}, u32[]{:S(2)}) collective-permute-start(bf16[12,128,128]{2,1,0:T(8,128)(2,1)S(1)} %get-tuple-element.9), channel_id=1, source_target_pairs={{16,32},{24,40},{48,64},{56,72},{80,96},{88,104},{112,128},{120,13... | collective-permute-start | bytes 1179656 | tf_op jit(solution)/shard_map/ppermute | solution.py:357
  72.9 10.1 %inner.1 = (bf16[12,128,128]{2,1,0:T(8,128)(2,1)S(1)}, bf16[8,2,128,128]{3,2,1,0:T(8,128)(2,1)S(1)}, f32[2,1024,128]{2,1,0:T(8,128)S(1)}) custom-call(f32[101]{0:T(128)S(1)} %pad_maximum_fusion.info_ref.bias_ref, bf16[16,4,128,128]{3,2,1,0:T(8,128)(2,1)S(1)} %all-to-all-done.x_ref), custom_call_target="tpu_custom_call" | custom-call | flops 1258291200 | bytes 5242880 | tf_op jit(solution)/shard_map/inner/pallas_call | solution.py:232
  83.0 0.0 collective-permute-done.first_ref
  83.0 0.0 collective-permute-done.1.second_ref
  83.0 4.9 %outer.1 = bf16[16,3,128,128]{3,2,1,0:T(8,128)(2,1)S(1)} custom-call(f32[101]{0:T(128)S(1)} %pad_maximum_fusion.info_ref.bias_ref, bf16[16,4,128,128]{3,2,1,0:T(8,128)(2,1)S(1)} %all-to-all-done.x_ref, bf16[12,128,128]{2,1,0:T(8,128)(2,1)S(1)} %collective-permute-done.first_ref, bf16[12,128,128]{2,1,0:T(8,128)(2,1)S(1)} %collective-permute-done.1.second_ref, ...), custom_call_target="tpu_custom_call" | custom-call | flops 671088640 | bytes 6291456 | tf_op jit(solution)/shard_map/outer/pallas_call | solution.py:319
  87.9 43.8 %all_to_all.10.in_ref = bf16[16,3,128,128]{3,2,1,0:T(8,128)(2,1)S(1)} all-to-all(bf16[16,3,128,128]{3,2,1,0:T(8,128)(2,1)S(1)} %outer.1), channel_id=1, replica_groups={{0,1,2,3,4,5,6,7,8,9,10,11,12,13,14,15},{16,17,18,19,20,21,22,23,24,25,..., dimensions={0} | all-to-all | bytes 3145728 | tf_op jit(solution)/shard_map/all_to_all | solution.py:353
  131.6 1.5 %unpack.1 = (bf16[128,2048]{1,0:T(8,128)(2,1)}, bf16[128,2048]{1,0:T(8,128)(2,1)}, bf16[128,2048]{1,0:T(8,128)(2,1)}) custom-call(bf16[16,3,128,128]{3,2,1,0:T(8,128)(2,1)S(1)} %all_to_all.10.in_ref), custom_call_target="tpu_custom_call" | custom-call | bytes 3145728 | tf_op jit(solution)/shard_map/unpack/pallas_call | solution.py:82
  (5 shorter events, 0.1 us)
Async XLA Ops:
  3.6 7.8 %copy-start = (s32[512,2]{0,1:T(2,128)S(1)}, s32[512,2]{0,1:T(2,128)}, u32[]{:S(2)}) copy-start(s32[512,2]{0,1:T(2,128)} %param.10) | copy-start | bytes 12292
  3.6 7.9 %copy-start.1 = (s32[512]{0:T(512)S(1)}, s32[512]{0:T(512)}, u32[]{:S(2)}) copy-start(s32[512]{0:T(512)} %param.11) | copy-start | bytes 6148
  3.6 55.5 %all-to-all-start = ((bf16[16,4,128,128]{3,2,1,0:T(8,128)(2,1)}), bf16[16,4,128,128]{3,2,1,0:T(8,128)(2,1)S(1)}, u32[]{:S(2)}, u32[]{:S(2)}) async-start(bf16[16,4,128,128]{3,2,1,0:T(8,128)(2,1)} %pack.1), calls=%async_computation | async-start | bytes 4194304 | tf_op jit(solution)/shard_map/all_to_all | solution.py:353
  59.8 23.2 %collective-permute-start = (bf16[12,128,128]{2,1,0:T(8,128)(2,1)S(1)}, bf16[12,128,128]{2,1,0:T(8,128)(2,1)S(1)}, u32[]{:S(2)}, u32[]{:S(2)}) collective-permute-start(bf16[12,128,128]{2,1,0:T(8,128)(2,1)S(1)} %get-tuple-element.8), channel_id=1, source_target_pairs={{0,16},{8,24},{32,48},{40,56},{64,80},{72,88},{96,112},{104,120},{... | collective-permute-start | bytes 1179656 | tf_op jit(solution)/shard_map/ppermute | solution.py:357
  63.8 19.2 %collective-permute-start.1 = (bf16[12,128,128]{2,1,0:T(8,128)(2,1)S(1)}, bf16[12,128,128]{2,1,0:T(8,128)(2,1)S(1)}, u32[]{:S(2)}, u32[]{:S(2)}) collective-permute-start(bf16[12,128,128]{2,1,0:T(8,128)(2,1)S(1)} %get-tuple-element.9), channel_id=1, source_target_pairs={{16,32},{24,40},{48,64},{56,72},{80,96},{88,104},{112,128},{120,13... | collective-permute-start | bytes 1179656 | tf_op jit(solution)/shard_map/ppermute | solution.py:357

commit v3 on v2

--- a/solution.py
+++ b/solution.py
@@ -13,8 +13,7 @@
 WINDOW = 2 * REACH + 1
 SPAN = WINDOW * TILE
 SCALE = float(HEAD_DIM) ** (-0.5)
-AXES = ("seq", "blk")
-CORES = 2
+CHUNKS = 2
 VMEM = pl.BlockSpec(memory_space=pltpu.VMEM)
 NT = (((1,), (1,)), ((), ()))
 TN = (((0,), (0,)), ((), ()))
@@ -24,15 +23,16 @@
     return pl.CostEstimate(flops=flops, bytes_accessed=moved, transcendentals=exps)
 
 
-def pack(arrays, peers):
+def pack(arrays, chunk, peers, after=()):
     rows, count = arrays[0].shape[0], len(arrays)
 
     def body(*refs):
-        ins, refs = refs[:count], refs[count:]
+        ins, refs = refs[:count], refs[count + len(after):]
         out_ref, held, in_sem, out_sem = refs
         reads = [
             [
-                pltpu.make_async_copy(ins[n].at[:, pl.ds(b * LANES, LANES)], held.at[b, n], in_sem.at[b, n])
+                pltpu.make_async_copy(
+                    ins[n].at[:, pl.ds((chunk * peers + b) * LANES, LANES)], held.at[b, n], in_sem.at[b, n])
                 for n in range(count)
             ]
             for b in range(peers)
@@ -51,7 +51,7 @@
     shape = (peers, count, rows, LANES)
     return pl.pallas_call(
         body,
-        in_specs=[pl.BlockSpec(memory_space=pl.ANY)] * count,
+        in_specs=[pl.BlockSpec(memory_space=pl.ANY)] * (count + len(after)),
         out_specs=pl.BlockSpec(memory_space=pl.ANY),
         out_shape=jax.ShapeDtypeStruct(shape, jnp.bfloat16),
         scratch_shapes=[
@@ -61,16 +61,18 @@
         ],
         cost_estimate=cost(0, 2 * peers * count * rows * LANES * 2),
         name="pack",
-    )(*arrays)
-
-
-def unpack(grads):
+    )(*arrays, *after)
+
+
+def unpack(grads, chunk, columns, so_far=None):
     peers, count, rows, _ = grads.shape
+    given = [] if so_far is None else list(so_far)
 
     def body(in_ref, *refs):
-        outs, sem = refs[:count], refs[count]
+        outs, sem = refs[len(given):len(given) + count], refs[len(given) + count]
         copies = [
-            pltpu.make_async_copy(in_ref.at[b, n], outs[n].at[:, pl.ds(b * LANES, LANES)], sem.at[b, n])
+            pltpu.make_async_copy(
+                in_ref.at[b, n], outs[n].at[:, pl.ds((chunk * peers + b) * LANES, LANES)], sem.at[b, n])
             for b in range(peers)
             for n in range(count)
         ]
@@ -79,16 +81,18 @@
         for copy in copies:
             copy.wait()
 
+    hbm = pl.BlockSpec(memory_space=pl.ANY)
     return pl.pallas_call(
         body,
-        in_specs=[pl.BlockSpec(memory_space=pl.ANY)],
-        out_specs=[pl.BlockSpec(memory_space=pl.ANY)] * count,
-        out_shape=[jax.ShapeDtypeStruct((rows, peers * LANES), jnp.bfloat16)] * count,
+        in_specs=[hbm] * (1 + len(given)),
+        out_specs=[hbm] * count,
+        out_shape=[jax.ShapeDtypeStruct((rows, columns), jnp.bfloat16)] * count,
         scratch_shapes=[pltpu.SemaphoreType.DMA((peers, count))],
+        input_output_aliases={1 + n: n for n in range(len(given))},
         compiler_params=pltpu.CompilerParams(vmem_limit_bytes=4 << 20),
         cost_estimate=cost(0, 2 * peers * count * rows * LANES * 2),
         name="unpack",
-    )(grads)
+    )(grads, *given)
 
 
 def rim_body(info_ref, x_ref, first_ref, second_ref):
@@ -168,15 +172,13 @@
     return (jnp.where(first, both[:TILE], both[TILE:]) * SCALE).astype(jnp.bfloat16)
 
 
-def inner_body(bias_ref, x_ref, dquery_ref, mid_ref, edge_ref, key_ref, value_ref, dkey_ref, dvalue_ref, *held):
+def inner_body(bias_ref, x_ref, dquery_ref, edge_ref, key_ref, value_ref, *held):
     tiles = x_ref.shape[0]
-    deep = 2 * REACH
     held = (held[:6], held[6:])
     for t in range(tiles):
         key_ref[t * TILE:(t + 1) * TILE] = x_ref[t, 1]
         value_ref[t * TILE:(t + 1) * TILE] = x_ref[t, 2]
-    dkey_ref[...] = jnp.zeros_like(dkey_ref)
-    dvalue_ref[...] = jnp.zeros_like(dvalue_ref)
+    edge_ref[...] = jnp.zeros_like(edge_ref)
 
     def rows_of(n):
         return pl.ds(n * TILE if isinstance(n, int) else pl.multiple_of(n * TILE, TILE), SPAN)
@@ -190,8 +192,8 @@
         _, _, query_ref, grad_ref, probs_ref, dscores_ref = held[slot]
         rows = rows_of(n)
         dscores = dscores_ref[...]
-        dkey_ref[rows] += jnp.dot(dscores, query_ref[...], preferred_element_type=jnp.float32)
-        dvalue_ref[rows] += jnp.dot(probs_ref[...], grad_ref[...], preferred_element_type=jnp.float32)
+        edge_ref[0, rows] += jnp.dot(dscores, query_ref[...], preferred_element_type=jnp.float32)
+        edge_ref[1, rows] += jnp.dot(probs_ref[...], grad_ref[...], preferred_element_type=jnp.float32)
         dquery_ref[n] = query_grad(dscores, key_ref[rows])
 
     steps = tiles - 2 * REACH
@@ -213,16 +215,6 @@
     end(steps - 2, 0)
     softmax_stage(held[1])
     end(steps - 1, 1)
-    for n, ref in ((0, dkey_ref), (1, dvalue_ref)):
-        for t in range(tiles):
-            block = ref[t * TILE:(t + 1) * TILE]
-            if t < deep:
-                edge_ref[n, t * TILE:(t + 1) * TILE] = block
-            elif t >= tiles - deep:
-                at = (t - tiles + 2 * deep) * TILE
-                edge_ref[n, at:at + TILE] = block
-            else:
-                mid_ref[t - deep, n] = block.astype(jnp.bfloat16)
 
 
 def inner(bias, taken):
@@ -232,14 +224,12 @@
     return pl.pallas_call(
         inner_body,
         in_specs=[pl.BlockSpec(memory_space=pltpu.SMEM), VMEM],
-        out_specs=[VMEM] * 3,
+        out_specs=[VMEM] * 2,
         out_shape=[
             jax.ShapeDtypeStruct((steps, TILE, LANES), jnp.bfloat16),
-            jax.ShapeDtypeStruct((tiles - 4 * REACH, 2, TILE, LANES), jnp.bfloat16),
-            jax.ShapeDtypeStruct((2, 4 * REACH * TILE, LANES), jnp.float32),
+            jax.ShapeDtypeStruct((2, whole, LANES), jnp.float32),
         ],
-        scratch_shapes=[pltpu.VMEM((whole, LANES), jnp.bfloat16)] * 2 + [pltpu.VMEM((whole, LANES), jnp.float32)] * 2
-        + held_shapes() * 2,
+        scratch_shapes=[pltpu.VMEM((whole, LANES), jnp.bfloat16)] * 2 + held_shapes() * 2,
         compiler_params=pltpu.CompilerParams(vmem_limit_bytes=28 << 20),
         cost_estimate=cost(steps * WINDOW * 10 * TILE * TILE * LANES, 5 << 20, steps * WINDOW * 2 * TILE * TILE),
         name="inner",
@@ -247,7 +237,7 @@
 
 
 def outer_body(
-    bias_ref, x_ref, first_ref, second_ref, dquery_ref, mid_ref, edge_ref, out_ref, halo_ref, key_ref, value_ref, acc_ref, *held
+    bias_ref, x_ref, first_ref, second_ref, dquery_ref, edge_ref, out_ref, halo_ref, key_ref, value_ref, acc_ref, *held
 ):
     tiles = x_ref.shape[0]
     deep = 2 * REACH
@@ -265,9 +255,6 @@
     acc_ref[...] = edge_ref[...]
     for t in range(tiles - 2 * REACH):
         out_ref[REACH + t, 0] = dquery_ref[t]
-    for t in range(tiles - 2 * deep):
-        out_ref[deep + t, 1] = mid_ref[t, 0]
-        out_ref[deep + t, 2] = mid_ref[t, 1]
 
     def place(step):
         j, high = step // 2, step % 2 == 1
@@ -313,12 +300,12 @@
             out_ref[tile, 1 + n] = acc_ref[n, t * TILE:(t + 1) * TILE].astype(jnp.bfloat16)
 
 
-def outer(bias, taken, first, second, dquery, mid, edge):
+def outer(bias, taken, first, second, dquery, edge):
     tiles = taken.shape[0]
     steps = 4 * REACH
     return pl.pallas_call(
         outer_body,
-        in_specs=[pl.BlockSpec(memory_space=pltpu.SMEM)] + [VMEM] * 6,
+        in_specs=[pl.BlockSpec(memory_space=pltpu.SMEM)] + [VMEM] * 5,
         out_specs=VMEM,
         out_shape=jax.ShapeDtypeStruct((tiles, 3, TILE, LANES), jnp.bfloat16),
         scratch_shapes=[pltpu.VMEM((2,) + first.shape, jnp.bfloat16)]
@@ -328,7 +315,7 @@
         compiler_params=pltpu.CompilerParams(vmem_limit_bytes=28 << 20),
         cost_estimate=cost(steps * WINDOW * 8 * TILE * TILE * LANES, 6 << 20, steps * WINDOW * 2 * TILE * TILE),
         name="outer",
-    )(bias, taken, first, second, dquery, mid, edge)
+    )(bias, taken, first, second, dquery, edge)
 
 
 def tile_bias(near_mask, motion_count, first, tiles):
@@ -345,31 +332,35 @@
 
 
 def per_device(query_states, key_states, value_states, output_grad, near_mask, motion_count):
-    blocks, spans = lax.axis_size("blk"), lax.axis_size("seq")
-    tiles = CORES * blocks
-    groups = [[g * tiles + t for t in range(tiles)] for g in range(spans // CORES)]
+    tiles, groups = lax.axis_size("blk"), lax.axis_size("seq")
+    columns = query_states.shape[1]
+    arrays = (query_states, key_states, value_states, output_grad)
 
     def exchange(x):
-        return lax.all_to_all(x, AXES, split_axis=0, concat_axis=0, tiled=True, axis_index_groups=groups)
+        return lax.all_to_all(x, "blk", split_axis=0, concat_axis=0, tiled=True)
 
     def swap(x, parity):
-        right = [(i, i + CORES) for i in range(spans - CORES) if i // CORES % 2 == parity]
+        right = [(i, i + 1) for i in range(groups - 1) if i % 2 == parity]
         return lax.ppermute(x, "seq", right + [(j, i) for i, j in right])
 
-    bias = tile_bias(near_mask, motion_count, lax.axis_index("seq") // CORES * tiles, tiles)
-    packed = pack((query_states, key_states, value_states, output_grad), tiles)
-    taken = exchange(packed)
-    first, second = rims(bias, taken)
-    first = swap(first, 0)
-    second = swap(second, 1)
-    parts = inner(bias, taken)
-    out = outer(bias, taken, first, second, *parts)
-    back = exchange(out)
-    return tuple(unpack(back))
+    taken, results = [], None
+    bias = tile_bias(near_mask, motion_count, lax.axis_index("seq") * tiles, tiles)
+    for c in range(CHUNKS):
+        packed = pack(arrays, c, tiles, (bias,) if c else ())
+        taken.append(exchange(packed))
+    for c in range(CHUNKS):
+        first, second = rims(bias, taken[c])
+        first = swap(first, 0)
+        second = swap(second, 1)
+        parts = inner(bias, taken[c])
+        out = outer(bias, taken[c], first, second, *parts)
+        back = exchange(out)
+        results = unpack(back, c, columns, results)
+    return tuple(results)
 
 
 def solution(mesh):
-    spec = P(AXES, None)
+    spec = P(("seq", "blk"), None)
     return jax.shard_map(
         per_device, mesh=mesh, in_specs=(spec,) * 4 + (P(), P()), out_specs=(spec,) * 3, check_vma=False
     )

time: 135 us -> 128 us (0.948)
  the two profiles are of different devices: /device:TPU:7 before, /device:TPU:453 now
where the time goes in v3:
time: 128 us; the launch traced here: 127 us
  waiting for transfers between devices  72.4 us (57%)
  starting transfers between devices  26.3 us (21%)
  Pallas kernels  25.7 us (20%)
    all_to_all x4, waiting for transfers between devices, exchange(): return lax.all_to_all(x, 'blk', split_axis=0, concat_axis=0, tiled=True)  60.1 us
    all_to_all x4, starting transfers between devices, exchange(): return lax.all_to_all(x, 'blk', split_axis=0, concat_axis=0, tiled=True)  17.5 us
    ppermute x4, waiting for transfers between devices, swap(): return lax.ppermute(x, 'seq', right + [(j, i) for i, j in right])  12.2 us
    pallas_call x2, Pallas kernels, outer(): pl.pallas_call(outer_body, in_specs=[pl.BlockSpec(memory_space=pltpu.SMEM...  11.4 us
    ppermute x4, starting transfers between devices, swap(): return lax.ppermute(x, 'seq', right + [(j, i) for i, j in right])  8.82 us
    pallas_call x2, Pallas kernels, inner(): pl.pallas_call(inner_body, in_specs=[pl.BlockSpec(memory_space=pltpu.SMEM...  6.57 us
    pallas_call x2, Pallas kernels, pack(): pl.pallas_call(body, in_specs=[pl.BlockSpec(memory_space=pl.ANY)] * (coun...  4.45 us
  transfers between devices with their start and end apart: 8, of which 6 were waited for; matrix products, arithmetic and copies ran while one was open for 1% of the time, Pallas kernels for 18%

profile of v3, /device:TPU:453, one launch (start us, length us, event | category | flops | bytes accessed | tf_op | source)
XLA Modules:
  0.0 127.1 jit_solution(16479333464813707985)
XLA Ops:
  0.6 2.2 %pack.3 = bf16[8,4,128,128]{3,2,1,0:T(8,128)(2,1)} custom-call(bf16[128,2048]{1,0:T(8,128)(2,1)} %refs_0_.3, bf16[128,2048]{1,0:T(8,128)(2,1)} %refs_1_.3, bf16[128,2048]{1,0:T(8,128)(2,1)} %refs_2_.3, bf16[128,2048]{1,0:T(8,128)(2,1)} %refs_3_.3), custom_call_target="tpu_custom_call" | custom-call | bytes 2097152 | tf_op jit(solution)/shard_map/pack/pallas_call | solution.py:52
  2.9 6.8 %all-to-all-start.2 = ((bf16[8,4,128,128]{3,2,1,0:T(8,128)(2,1)}), bf16[8,4,128,128]{3,2,1,0:T(8,128)(2,1)S(1)}, u32[]{:S(2)}, u32[]{:S(2)}) async-start(bf16[8,4,128,128]{3,2,1,0:T(8,128)(2,1)} %pack.3), calls=%async_computation.2 | async-start | bytes 2097152 | tf_op jit(solution)/shard_map/all_to_all | solution.py:340
  9.7 0.0 copy-start.2
  9.7 0.0 copy-start.1
  9.8 0.6 copy-done.2
  10.4 0.1 compare_bitcast_fusion
  10.5 0.0 copy-done.1
  10.5 0.1 fusion.3
  10.6 0.1 fusion.2
  10.7 0.1 copy.13
  10.8 0.1 reshape.27
  10.9 0.6 pad_maximum_fusion.refs_4_.info_ref.bias_ref
  11.5 2.2 %pack.2 = bf16[8,4,128,128]{3,2,1,0:T(8,128)(2,1)} custom-call(bf16[128,2048]{1,0:T(8,128)(2,1)} %refs_0_.3, bf16[128,2048]{1,0:T(8,128)(2,1)} %refs_1_.3, bf16[128,2048]{1,0:T(8,128)(2,1)} %refs_2_.3, bf16[128,2048]{1,0:T(8,128)(2,1)} %refs_3_.3, f32[61]{0:T(128)} %pad_maximum_fusion.refs_4_.info_ref.bias_ref), custom_call_target="tpu_custom_call" | custom-call | bytes 2097152 | tf_op jit(solution)/shard_map/pack/pallas_call | solution.py:52
  13.7 0.0 copy-start
  13.7 25.2 %all-to-all-done.2.x_ref = bf16[8,4,128,128]{3,2,1,0:T(8,128)(2,1)S(1)} async-done(((bf16[8,4,128,128]{3,2,1,0:T(8,128)(2,1)}), bf16[8,4,128,128]{3,2,1,0:T(8,128)(2,1)S(1)}, u32[]{:S(2)}, u32[]{:S(2)}) %all-to-all-start.2) | async-done | bytes 1048608 | tf_op jit(solution)/shard_map/all_to_all | solution.py:340
  38.9 3.6 %all-to-all-start = ((bf16[8,4,128,128]{3,2,1,0:T(8,128)(2,1)}), bf16[8,4,128,128]{3,2,1,0:T(8,128)(2,1)S(1)}, u32[]{:S(2)}, u32[]{:S(2)}) async-start(bf16[8,4,128,128]{3,2,1,0:T(8,128)(2,1)} %pack.2), calls=%async_computation | async-start | bytes 2097152 | tf_op jit(solution)/shard_map/all_to_all | solution.py:340
  42.5 0.0 copy-done
  42.5 0.6 rims.3
  43.1 2.4 %collective-permute-start.2 = (bf16[12,128,128]{2,1,0:T(8,128)(2,1)S(1)}, bf16[12,128,128]{2,1,0:T(8,128)(2,1)S(1)}, u32[]{:S(2)}, u32[]{:S(2)}) collective-permute-start(bf16[12,128,128]{2,1,0:T(8,128)(2,1)S(1)} %get-tuple-element.18), channel_id=1, source_target_pairs={{0,8},{16,24},{32,40},{48,56},{64,72},{80,88},{96,104},{112,120},{... | collective-permute-start | bytes 1179656 | tf_op jit(solution)/shard_map/ppermute | solution.py:344
  45.5 1.9 %collective-permute-start.3 = (bf16[12,128,128]{2,1,0:T(8,128)(2,1)S(1)}, bf16[12,128,128]{2,1,0:T(8,128)(2,1)S(1)}, u32[]{:S(2)}, u32[]{:S(2)}) collective-permute-start(bf16[12,128,128]{2,1,0:T(8,128)(2,1)S(1)} %get-tuple-element.19), channel_id=1, source_target_pairs={{8,16},{24,32},{40,48},{56,64},{72,80},{88,96},{104,112},{120,128}... | collective-permute-start | bytes 1179656 | tf_op jit(solution)/shard_map/ppermute | solution.py:344
  47.4 3.3 %inner.3 = (bf16[4,128,128]{2,1,0:T(8,128)(2,1)S(1)}, f32[2,1024,128]{2,1,0:T(8,128)S(1)}) custom-call(f32[61]{0:T(128)S(1)} %copy-done, bf16[8,4,128,128]{3,2,1,0:T(8,128)(2,1)S(1)} %all-to-all-done.2.x_ref), custom_call_target="tpu_custom_call" | custom-call | flops 419430400 | bytes 5242880 | tf_op jit(solution)/shard_map/inner/pallas_call | solution.py:224
  50.7 0.0 collective-permute-done.2.first_ref
  50.7 6.1 %collective-permute-done.3.second_ref = bf16[12,128,128]{2,1,0:T(8,128)(2,1)S(1)} collective-permute-done((bf16[12,128,128]{2,1,0:T(8,128)(2,1)S(1)}, bf16[12,128,128]{2,1,0:T(8,128)(2,1)S(1)}, u32[]{:S(2)}, u32[]{:S(2)}) %collective-permute-start.3) | collective-permute-done | bytes 393248 | tf_op jit(solution)/shard_map/ppermute | solution.py:344
  56.8 5.7 %outer.3 = bf16[8,3,128,128]{3,2,1,0:T(8,128)(2,1)} custom-call(f32[61]{0:T(128)S(1)} %copy-done, bf16[8,4,128,128]{3,2,1,0:T(8,128)(2,1)S(1)} %all-to-all-done.2.x_ref, bf16[12,128,128]{2,1,0:T(8,128)(2,1)S(1)} %collective-permute-done.2.first_ref, bf16[12,128,128]{2,1,0:T(8,128)(2,1)S(1)} %collective-permute-done.3.second_ref, ...), custom_call_target="tpu_custom_call" | custom-call | flops 671088640 | bytes 6291456 | tf_op jit(solution)/shard_map/outer/pallas_call | solution.py:306
  62.5 9.1 %all-to-all-done.x_ref = bf16[8,4,128,128]{3,2,1,0:T(8,128)(2,1)S(1)} async-done(((bf16[8,4,128,128]{3,2,1,0:T(8,128)(2,1)}), bf16[8,4,128,128]{3,2,1,0:T(8,128)(2,1)S(1)}, u32[]{:S(2)}, u32[]{:S(2)}) %all-to-all-start) | async-done | bytes 1048608 | tf_op jit(solution)/shard_map/all_to_all | solution.py:340
  71.6 3.5 %all-to-all-start.3 = ((bf16[8,3,128,128]{3,2,1,0:T(8,128)(2,1)}), bf16[8,3,128,128]{3,2,1,0:T(8,128)(2,1)S(1)}, u32[]{:S(2)}, u32[]{:S(2)}) async-start(bf16[8,3,128,128]{3,2,1,0:T(8,128)(2,1)} %outer.3), calls=%async_computation.3 | async-start | bytes 1572864 | tf_op jit(solution)/shard_map/all_to_all | solution.py:340
  75.2 0.6 rims.2
  75.8 2.4 %collective-permute-start = (bf16[12,128,128]{2,1,0:T(8,128)(2,1)S(1)}, bf16[12,128,128]{2,1,0:T(8,128)(2,1)S(1)}, u32[]{:S(2)}, u32[]{:S(2)}) collective-permute-start(bf16[12,128,128]{2,1,0:T(8,128)(2,1)S(1)} %get-tuple-element.14), channel_id=1, source_target_pairs={{0,8},{16,24},{32,40},{48,56},{64,72},{80,88},{96,104},{112,120},{... | collective-permute-start | bytes 1179656 | tf_op jit(solution)/shard_map/ppermute | solution.py:344
  78.2 2.1 %collective-permute-start.1 = (bf16[12,128,128]{2,1,0:T(8,128)(2,1)S(1)}, bf16[12,128,128]{2,1,0:T(8,128)(2,1)S(1)}, u32[]{:S(2)}, u32[]{:S(2)}) collective-permute-start(bf16[12,128,128]{2,1,0:T(8,128)(2,1)S(1)} %get-tuple-element.15), channel_id=1, source_target_pairs={{8,16},{24,32},{40,48},{56,64},{72,80},{88,96},{104,112},{120,128}... | collective-permute-start | bytes 1179656 | tf_op jit(solution)/shard_map/ppermute | solution.py:344
  80.3 3.3 %inner.2 = (bf16[4,128,128]{2,1,0:T(8,128)(2,1)S(1)}, f32[2,1024,128]{2,1,0:T(8,128)S(1)}) custom-call(f32[61]{0:T(128)S(1)} %copy-done, bf16[8,4,128,128]{3,2,1,0:T(8,128)(2,1)S(1)} %all-to-all-done.x_ref), custom_call_target="tpu_custom_call" | custom-call | flops 419430400 | bytes 5242880 | tf_op jit(solution)/shard_map/inner/pallas_call | solution.py:224
  83.6 0.0 collective-permute-done.first_ref
  83.6 6.1 %collective-permute-done.1.second_ref = bf16[12,128,128]{2,1,0:T(8,128)(2,1)S(1)} collective-permute-done((bf16[12,128,128]{2,1,0:T(8,128)(2,1)S(1)}, bf16[12,128,128]{2,1,0:T(8,128)(2,1)S(1)}, u32[]{:S(2)}, u32[]{:S(2)}) %collective-permute-start.1) | collective-permute-done | bytes 393248 | tf_op jit(solution)/shard_map/ppermute | solution.py:344
  89.7 5.7 %outer.2 = bf16[8,3,128,128]{3,2,1,0:T(8,128)(2,1)} custom-call(f32[61]{0:T(128)S(1)} %copy-done, bf16[8,4,128,128]{3,2,1,0:T(8,128)(2,1)S(1)} %all-to-all-done.x_ref, bf16[12,128,128]{2,1,0:T(8,128)(2,1)S(1)} %collective-permute-done.first_ref, bf16[12,128,128]{2,1,0:T(8,128)(2,1)S(1)} %collective-permute-done.1.second_ref, ...), custom_call_target="tpu_custom_call" | custom-call | flops 671088640 | bytes 6291456 | tf_op jit(solution)/shard_map/outer/pallas_call | solution.py:306
  95.4 3.3 %all-to-all-done.3.in_ref = bf16[8,3,128,128]{3,2,1,0:T(8,128)(2,1)S(1)} async-done(((bf16[8,3,128,128]{3,2,1,0:T(8,128)(2,1)}), bf16[8,3,128,128]{3,2,1,0:T(8,128)(2,1)S(1)}, u32[]{:S(2)}, u32[]{:S(2)}) %all-to-all-start.3) | async-done | bytes 786464 | tf_op jit(solution)/shard_map/all_to_all | solution.py:340
  98.7 3.6 %all-to-all-start.1 = ((bf16[8,3,128,128]{3,2,1,0:T(8,128)(2,1)}), bf16[8,3,128,128]{3,2,1,0:T(8,128)(2,1)S(1)}, u32[]{:S(2)}, u32[]{:S(2)}) async-start(bf16[8,3,128,128]{3,2,1,0:T(8,128)(2,1)} %outer.2), calls=%async_computation.1 | async-start | bytes 1572864 | tf_op jit(solution)/shard_map/all_to_all | solution.py:340
  102.2 1.1 unpack.2
  103.3 22.6 %all-to-all-done.1.in_ref = bf16[8,3,128,128]{3,2,1,0:T(8,128)(2,1)S(1)} async-done(((bf16[8,3,128,128]{3,2,1,0:T(8,128)(2,1)}), bf16[8,3,128,128]{3,2,1,0:T(8,128)(2,1)S(1)}, u32[]{:S(2)}, u32[]{:S(2)}) %all-to-all-start.1) | async-done | bytes 786464 | tf_op jit(solution)/shard_map/all_to_all | solution.py:340
  125.9 1.1 unpack.3
  (5 shorter events, 0.1 us)
Async XLA Ops:
  2.9 36.0 %all-to-all-start.2 = ((bf16[8,4,128,128]{3,2,1,0:T(8,128)(2,1)}), bf16[8,4,128,128]{3,2,1,0:T(8,128)(2,1)S(1)}, u32[]{:S(2)}, u32[]{:S(2)}) async-start(bf16[8,4,128,128]{3,2,1,0:T(8,128)(2,1)} %pack.3), calls=%async_computation.2 | async-start | bytes 2097152 | tf_op jit(solution)/shard_map/all_to_all | solution.py:340
  9.7 0.7 copy-start.2
  9.7 0.7 copy-start.1
  13.7 28.8 %copy-start = (f32[61]{0:T(128)S(1)}, f32[61]{0:T(128)}, u32[]{:S(2)}) copy-start(f32[61]{0:T(128)} %pad_maximum_fusion.refs_4_.info_ref.bias_ref) | copy-start | bytes 736
  38.9 32.7 %all-to-all-start = ((bf16[8,4,128,128]{3,2,1,0:T(8,128)(2,1)}), bf16[8,4,128,128]{3,2,1,0:T(8,128)(2,1)S(1)}, u32[]{:S(2)}, u32[]{:S(2)}) async-start(bf16[8,4,128,128]{3,2,1,0:T(8,128)(2,1)} %pack.2), calls=%async_computation | async-start | bytes 2097152 | tf_op jit(solution)/shard_map/all_to_all | solution.py:340
  43.1 7.6 %collective-permute-start.2 = (bf16[12,128,128]{2,1,0:T(8,128)(2,1)S(1)}, bf16[12,128,128]{2,1,0:T(8,128)(2,1)S(1)}, u32[]{:S(2)}, u32[]{:S(2)}) collective-permute-start(bf16[12,128,128]{2,1,0:T(8,128)(2,1)S(1)} %get-tuple-element.18), channel_id=1, source_target_pairs={{0,8},{16,24},{32,40},{48,56},{64,72},{80,88},{96,104},{112,120},{... | collective-permute-start | bytes 1179656 | tf_op jit(solution)/shard_map/ppermute | solution.py:344
  45.5 11.3 %collective-permute-start.3 = (bf16[12,128,128]{2,1,0:T(8,128)(2,1)S(1)}, bf16[12,128,128]{2,1,0:T(8,128)(2,1)S(1)}, u32[]{:S(2)}, u32[]{:S(2)}) collective-permute-start(bf16[12,128,128]{2,1,0:T(8,128)(2,1)S(1)} %get-tuple-element.19), channel_id=1, source_target_pairs={{8,16},{24,32},{40,48},{56,64},{72,80},{88,96},{104,112},{120,128}... | collective-permute-start | bytes 1179656 | tf_op jit(solution)/shard_map/ppermute | solution.py:344
  71.6 27.0 %all-to-all-start.3 = ((bf16[8,3,128,128]{3,2,1,0:T(8,128)(2,1)}), bf16[8,3,128,128]{3,2,1,0:T(8,128)(2,1)S(1)}, u32[]{:S(2)}, u32[]{:S(2)}) async-start(bf16[8,3,128,128]{3,2,1,0:T(8,128)(2,1)} %outer.3), calls=%async_computation.3 | async-start | bytes 1572864 | tf_op jit(solution)/shard_map/all_to_all | solution.py:340
  75.8 7.8 %collective-permute-start = (bf16[12,128,128]{2,1,0:T(8,128)(2,1)S(1)}, bf16[12,128,128]{2,1,0:T(8,128)(2,1)S(1)}, u32[]{:S(2)}, u32[]{:S(2)}) collective-permute-start(bf16[12,128,128]{2,1,0:T(8,128)(2,1)S(1)} %get-tuple-element.14), channel_id=1, source_target_pairs={{0,8},{16,24},{32,40},{48,56},{64,72},{80,88},{96,104},{112,120},{... | collective-permute-start | bytes 1179656 | tf_op jit(solution)/shard_map/ppermute | solution.py:344
  78.2 11.5 %collective-permute-start.1 = (bf16[12,128,128]{2,1,0:T(8,128)(2,1)S(1)}, bf16[12,128,128]{2,1,0:T(8,128)(2,1)S(1)}, u32[]{:S(2)}, u32[]{:S(2)}) collective-permute-start(bf16[12,128,128]{2,1,0:T(8,128)(2,1)S(1)} %get-tuple-element.15), channel_id=1, source_target_pairs={{8,16},{24,32},{40,48},{56,64},{72,80},{88,96},{104,112},{120,128}... | collective-permute-start | bytes 1179656 | tf_op jit(solution)/shard_map/ppermute | solution.py:344
  98.7 27.2 %all-to-all-start.1 = ((bf16[8,3,128,128]{3,2,1,0:T(8,128)(2,1)}), bf16[8,3,128,128]{3,2,1,0:T(8,128)(2,1)S(1)}, u32[]{:S(2)}, u32[]{:S(2)}) async-start(bf16[8,3,128,128]{3,2,1,0:T(8,128)(2,1)} %outer.2), calls=%async_computation.1 | async-start | bytes 1572864 | tf_op jit(solution)/shard_map/all_to_all | solution.py:340

commit v4 on v3

--- a/solution.py
+++ b/solution.py
@@ -14,6 +14,7 @@
 SPAN = WINDOW * TILE
 SCALE = float(HEAD_DIM) ** (-0.5)
 CHUNKS = 2
+ORDER = (4, 3, 5, 2, 6, 1, 7)
 VMEM = pl.BlockSpec(memory_space=pltpu.VMEM)
 NT = (((1,), (1,)), ((), ()))
 TN = (((0,), (0,)), ((), ()))
@@ -23,11 +24,11 @@
     return pl.CostEstimate(flops=flops, bytes_accessed=moved, transcendentals=exps)
 
 
-def pack(arrays, chunk, peers, after=()):
+def pack(arrays, chunk, peers):
     rows, count = arrays[0].shape[0], len(arrays)
 
     def body(*refs):
-        ins, refs = refs[:count], refs[count + len(after):]
+        ins, refs = refs[:count], refs[count:]
         out_ref, held, in_sem, out_sem = refs
         reads = [
             [
@@ -51,7 +52,7 @@
     shape = (peers, count, rows, LANES)
     return pl.pallas_call(
         body,
-        in_specs=[pl.BlockSpec(memory_space=pl.ANY)] * (count + len(after)),
+        in_specs=[pl.BlockSpec(memory_space=pl.ANY)] * count,
         out_specs=pl.BlockSpec(memory_space=pl.ANY),
         out_shape=jax.ShapeDtypeStruct(shape, jnp.bfloat16),
         scratch_shapes=[
@@ -61,7 +62,66 @@
         ],
         cost_estimate=cost(0, 2 * peers * count * rows * LANES * 2),
         name="pack",
-    )(*arrays, *after)
+    )(*arrays)
+
+
+def pack_around(arrays, chunk, peers, me):
+    rows, count = arrays[0].shape[0], len(arrays)
+
+    def body(me_ref, *refs):
+        ins, outs = refs[:count], refs[count:count + peers]
+        held, in_sem, out_sem = refs[count + peers:]
+        reads, writes = [], []
+        for b in range(peers):
+            at = pl.multiple_of((chunk * peers + (me_ref[0] + b) % peers) * LANES, LANES)
+            reads.append([
+                pltpu.make_async_copy(ins[n].at[:, pl.ds(at, LANES)], held.at[b, n], in_sem.at[b, n])
+                for n in range(count)
+            ])
+            writes.append(pltpu.make_async_copy(held.at[b], outs[b], out_sem.at[b]))
+        for b in range(peers):
+            for n in range(count):
+                reads[b][n].start()
+        for b in range(peers):
+            for n in range(count):
+                reads[b][n].wait()
+            writes[b].start()
+        for b in range(peers):
+            writes[b].wait()
+
+    block = (count, rows, LANES)
+    hbm = pl.BlockSpec(memory_space=pl.ANY)
+    return pl.pallas_call(
+        body,
+        in_specs=[pl.BlockSpec(memory_space=pltpu.SMEM)] + [hbm] * count,
+        out_specs=[hbm] * peers,
+        out_shape=[jax.ShapeDtypeStruct(block, jnp.bfloat16)] * peers,
+        scratch_shapes=[
+            pltpu.VMEM((peers,) + block, jnp.bfloat16),
+            pltpu.SemaphoreType.DMA((peers, count)),
+            pltpu.SemaphoreType.DMA((peers,)),
+        ],
+        cost_estimate=cost(0, 2 * peers * count * rows * LANES * 2),
+        name="pack_around",
+    )(me, *arrays)
+
+
+def join(blocks, me):
+    peers = len(blocks)
+
+    def body(me_ref, *refs):
+        for n in range(peers):
+            refs[peers][(me_ref[0] + peers - n) % peers] = refs[n][...]
+
+    return pl.pallas_call(
+        body,
+        in_specs=[pl.BlockSpec(memory_space=pltpu.SMEM)] + [VMEM] * peers,
+        out_specs=VMEM,
+        out_shape=jax.ShapeDtypeStruct((peers,) + blocks[0].shape, blocks[0].dtype),
+        compiler_params=pltpu.CompilerParams(vmem_limit_bytes=8 << 20),
+        cost_estimate=cost(0, 2 << 20),
+        name="join",
+    )(me, *blocks)
 
 
 def unpack(grads, chunk, columns, so_far=None):
@@ -331,6 +391,21 @@
     return jnp.concatenate([jnp.where(allowed, 0.0, -1e30).astype(jnp.float32).reshape(-1), odd[None]])
 
 
+def gate(table):
+    def body(in_ref, out_ref):
+        out_ref[...] = in_ref[...]
+
+    return pl.pallas_call(
+        body,
+        in_specs=[VMEM],
+        out_specs=VMEM,
+        out_shape=jax.ShapeDtypeStruct(table.shape, table.dtype),
+        compiler_params=pltpu.CompilerParams(vmem_limit_bytes=1 << 20),
+        cost_estimate=cost(0, 1 << 10),
+        name="gate",
+    )(table)
+
+
 def per_device(query_states, key_states, value_states, output_grad, near_mask, motion_count):
     tiles, groups = lax.axis_size("blk"), lax.axis_size("seq")
     columns = query_states.shape[1]
@@ -345,15 +420,20 @@
 
     taken, results = [], None
     bias = tile_bias(near_mask, motion_count, lax.axis_index("seq") * tiles, tiles)
+    me = lax.axis_index("blk").reshape(1)
+    packed = pack(arrays, 0, tiles)
+    taken.append(exchange(packed))
+    blocks = list(pack_around(arrays, 1, tiles, me))
+    for n in ORDER:
+        blocks[n] = lax.ppermute(blocks[n], "blk", [(i, (i + n) % tiles) for i in range(tiles)])
+    taken.append(join(blocks, me))
+    info = gate(bias)
     for c in range(CHUNKS):
-        packed = pack(arrays, c, tiles, (bias,) if c else ())
-        taken.append(exchange(packed))
-    for c in range(CHUNKS):
-        first, second = rims(bias, taken[c])
+        first, second = rims(info, taken[c])
         first = swap(first, 0)
         second = swap(second, 1)
-        parts = inner(bias, taken[c])
-        out = outer(bias, taken[c], first, second, *parts)
+        parts = inner(info, taken[c])
+        out = outer(info, taken[c], first, second, *parts)
         back = exchange(out)
         results = unpack(back, c, columns, results)
     return tuple(results)

time: 128 us -> 155 us (1.21)
  the two profiles are of different devices: /device:TPU:453 before, /device:TPU:449 now
where the time goes in v4:
time: 155 us; the launch traced here: 154 us
  waiting for transfers between devices  75 us (48%)
  starting transfers between devices  49.8 us (32%)
  Pallas kernels  25.8 us (17%)
  local copies, waits for them, and re-layouts  1.78 us (1%)
    all_to_all x3, waiting for transfers between devices, exchange(): return lax.all_to_all(x, 'blk', split_axis=0, concat_axis=0, tiled=True)  49.2 us
    ppermute x7, starting transfers between devices, per_device(): lax.ppermute(blocks[n], 'blk', [(i, (i + n) % tiles) for i in range(tiles)])  26.1 us
    all_to_all x3, starting transfers between devices, exchange(): return lax.all_to_all(x, 'blk', split_axis=0, concat_axis=0, tiled=True)  15.3 us
    ppermute x7, waiting for transfers between devices, per_device(): lax.ppermute(blocks[n], 'blk', [(i, (i + n) % tiles) for i in range(tiles)])  14 us
    ppermute x4, waiting for transfers between devices, swap(): return lax.ppermute(x, 'seq', right + [(j, i) for i, j in right])  11.8 us
    pallas_call x2, Pallas kernels, outer(): pl.pallas_call(outer_body, in_specs=[pl.BlockSpec(memory_space=pltpu.SMEM...  11.4 us
    ppermute x4, starting transfers between devices, swap(): return lax.ppermute(x, 'seq', right + [(j, i) for i, j in right])  8.34 us
    pallas_call x2, Pallas kernels, inner(): pl.pallas_call(inner_body, in_specs=[pl.BlockSpec(memory_space=pltpu.SMEM...  6.55 us
  transfers between devices with their start and end apart: 14, of which 9 were waited for; matrix products, arithmetic and copies ran while one was open for 0% of the time, Pallas kernels for 11%

profile of v4, /device:TPU:449, one launch (start us, length us, event | category | flops | bytes accessed | tf_op | source)
XLA Modules:
  0.0 153.7 jit_solution(7450836228156280384)
XLA Ops:
  0.6 2.2 %pack.1 = bf16[8,4,128,128]{3,2,1,0:T(8,128)(2,1)} custom-call(bf16[128,2048]{1,0:T(8,128)(2,1)} %refs_0_.3, bf16[128,2048]{1,0:T(8,128)(2,1)} %refs_1_.3, bf16[128,2048]{1,0:T(8,128)(2,1)} %refs_2_.3, bf16[128,2048]{1,0:T(8,128)(2,1)} %refs_3_.3), custom_call_target="tpu_custom_call" | custom-call | bytes 2097152 | tf_op jit(solution)/shard_map/pack/pallas_call | solution.py:53
  2.9 6.8 %all-to-all-start.1 = ((bf16[8,4,128,128]{3,2,1,0:T(8,128)(2,1)}), bf16[8,4,128,128]{3,2,1,0:T(8,128)(2,1)S(1)}, u32[]{:S(2)}, u32[]{:S(2)}) async-start(bf16[8,4,128,128]{3,2,1,0:T(8,128)(2,1)} %pack.1), calls=%async_computation.1 | async-start | bytes 2097152 | tf_op jit(solution)/shard_map/all_to_all | solution.py:415
  9.7 0.0 copy-start.1
  9.7 0.6 copy-done.2
  10.4 0.1 compare_bitcast_fusion
  10.5 0.1 fusion.3
  10.6 0.1 fusion.2
  10.7 0.1 copy.13
  10.8 0.1 reshape.31
  10.9 0.1 pad_maximum_fusion.in_ref
  11.0 27.9 %all-to-all-done.1.x_ref = bf16[8,4,128,128]{3,2,1,0:T(8,128)(2,1)S(1)} async-done(((bf16[8,4,128,128]{3,2,1,0:T(8,128)(2,1)}), bf16[8,4,128,128]{3,2,1,0:T(8,128)(2,1)S(1)}, u32[]{:S(2)}, u32[]{:S(2)}) %all-to-all-start.1) | async-done | bytes 1048608 | tf_op jit(solution)/shard_map/all_to_all | solution.py:415
  38.9 0.6 rims.3
  39.5 2.4 %collective-permute-start.9 = (bf16[12,128,128]{2,1,0:T(8,128)(2,1)S(1)}, bf16[12,128,128]{2,1,0:T(8,128)(2,1)S(1)}, u32[]{:S(2)}, u32[]{:S(2)}) collective-permute-start(bf16[12,128,128]{2,1,0:T(8,128)(2,1)S(1)} %get-tuple-element.34), channel_id=1, source_target_pairs={{0,8},{16,24},{32,40},{48,56},{64,72},{80,88},{96,104},{112,120},{... | collective-permute-start | bytes 1179656 | tf_op jit(solution)/shard_map/ppermute | solution.py:419
  41.9 1.9 %collective-permute-start.10 = (bf16[12,128,128]{2,1,0:T(8,128)(2,1)S(1)}, bf16[12,128,128]{2,1,0:T(8,128)(2,1)S(1)}, u32[]{:S(2)}, u32[]{:S(2)}) collective-permute-start(bf16[12,128,128]{2,1,0:T(8,128)(2,1)S(1)} %get-tuple-element.35), channel_id=1, source_target_pairs={{8,16},{24,32},{40,48},{56,64},{72,80},{88,96},{104,112},{120,128}... | collective-permute-start | bytes 1179656 | tf_op jit(solution)/shard_map/ppermute | solution.py:419
  43.8 3.3 %inner.3 = (bf16[4,128,128]{2,1,0:T(8,128)(2,1)S(1)}, f32[2,1024,128]{2,1,0:T(8,128)S(1)}) custom-call(f32[61]{0:T(128)S(1)} %gate.1.info_ref.bias_ref, bf16[8,4,128,128]{3,2,1,0:T(8,128)(2,1)S(1)} %all-to-all-done.1.x_ref), custom_call_target="tpu_custom_call" | custom-call | flops 419430400 | bytes 5242880 | tf_op jit(solution)/shard_map/inner/pallas_call | solution.py:284
  47.1 0.0 collective-permute-done.9.first_ref
  47.1 6.0 %collective-permute-done.10.second_ref = bf16[12,128,128]{2,1,0:T(8,128)(2,1)S(1)} collective-permute-done((bf16[12,128,128]{2,1,0:T(8,128)(2,1)S(1)}, bf16[12,128,128]{2,1,0:T(8,128)(2,1)S(1)}, u32[]{:S(2)}, u32[]{:S(2)}) %collective-permute-start.10) | collective-permute-done | bytes 393248 | tf_op jit(solution)/shard_map/ppermute | solution.py:419
  53.1 5.7 %outer.3 = bf16[8,3,128,128]{3,2,1,0:T(8,128)(2,1)} custom-call(f32[61]{0:T(128)S(1)} %gate.1.info_ref.bias_ref, bf16[8,4,128,128]{3,2,1,0:T(8,128)(2,1)S(1)} %all-to-all-done.1.x_ref, bf16[12,128,128]{2,1,0:T(8,128)(2,1)S(1)} %collective-permute-done.9.first_ref, bf16[12,128,128]{2,1,0:T(8,128)(2,1)S(1)} %collective-permute-done.10.second_ref, ...), custom_call_target="tpu_custom_call" | custom-call | flops 671088640 | bytes 6291456 | tf_op jit(solution)/shard_map/outer/pallas_call | solution.py:366
  58.8 3.5 %all-to-all-start.2 = ((bf16[8,3,128,128]{3,2,1,0:T(8,128)(2,1)}), bf16[8,3,128,128]{3,2,1,0:T(8,128)(2,1)S(1)}, u32[]{:S(2)}, u32[]{:S(2)}) async-start(bf16[8,3,128,128]{3,2,1,0:T(8,128)(2,1)} %outer.3), calls=%async_computation.2 | async-start | bytes 1572864 | tf_op jit(solution)/shard_map/all_to_all | solution.py:415
  62.3 2.2 %pack_around.1 = (bf16[4,128,128]{2,1,0:T(8,128)(2,1)}, bf16[4,128,128]{2,1,0:T(8,128)(2,1)}, bf16[4,128,128]{2,1,0:T(8,128)(2,1)}, bf16[4,128,128]{2,1,0:T(8,12...) custom-call(s32[1]{0:T(128)} %bitcast.2.me_ref, ...), custom_call_target="tpu_custom_call" | custom-call | bytes 2097152 | tf_op jit(solution)/shard_map/pack_around/pallas_call | solution.py:94
  64.6 3.2 %collective-permute-start = (bf16[4,128,128]{2,1,0:T(8,128)(2,1)}, bf16[4,128,128]{2,1,0:T(8,128)(2,1)S(1)}, u32[]{:S(2)}, u32[]{:S(2)}) collective-permute-start(bf16[4,128,128]{2,1,0:T(8,128)(2,1)} %get-tuple-element.23), channel_id=1, source_target_pairs={{0,1},{1,2},{2,3},{3,4},{4,5},{5,6},{6,7},{7,0},{8,9},{9,10},{10,1... | collective-permute-start | bytes 393224 | tf_op jit(solution)/shard_map/ppermute | solution.py:428
  67.8 4.0 %collective-permute-start.1 = (bf16[4,128,128]{2,1,0:T(8,128)(2,1)}, bf16[4,128,128]{2,1,0:T(8,128)(2,1)S(1)}, u32[]{:S(2)}, u32[]{:S(2)}) collective-permute-start(bf16[4,128,128]{2,1,0:T(8,128)(2,1)} %get-tuple-element.24), channel_id=1, source_target_pairs={{0,2},{1,3},{2,4},{3,5},{4,6},{5,7},{6,0},{7,1},{8,10},{9,11},{10,... | collective-permute-start | bytes 393224 | tf_op jit(solution)/shard_map/ppermute | solution.py:428
  71.8 4.3 %collective-permute-start.2 = (bf16[4,128,128]{2,1,0:T(8,128)(2,1)}, bf16[4,128,128]{2,1,0:T(8,128)(2,1)S(1)}, u32[]{:S(2)}, u32[]{:S(2)}) collective-permute-start(bf16[4,128,128]{2,1,0:T(8,128)(2,1)} %get-tuple-element.25), channel_id=1, source_target_pairs={{0,3},{1,4},{2,5},{3,6},{4,7},{5,0},{6,1},{7,2},{8,11},{9,12},{10,... | collective-permute-start | bytes 393224 | tf_op jit(solution)/shard_map/ppermute | solution.py:428
  76.2 4.0 %collective-permute-start.3 = (bf16[4,128,128]{2,1,0:T(8,128)(2,1)}, bf16[4,128,128]{2,1,0:T(8,128)(2,1)S(1)}, u32[]{:S(2)}, u32[]{:S(2)}) collective-permute-start(bf16[4,128,128]{2,1,0:T(8,128)(2,1)} %get-tuple-element.26), channel_id=1, source_target_pairs={{0,4},{1,5},{2,6},{3,7},{4,0},{5,1},{6,2},{7,3},{8,12},{9,13},{10,... | collective-permute-start | bytes 393224 | tf_op jit(solution)/shard_map/ppermute | solution.py:428
  80.1 4.3 %collective-permute-start.4 = (bf16[4,128,128]{2,1,0:T(8,128)(2,1)}, bf16[4,128,128]{2,1,0:T(8,128)(2,1)S(1)}, u32[]{:S(2)}, u32[]{:S(2)}) collective-permute-start(bf16[4,128,128]{2,1,0:T(8,128)(2,1)} %get-tuple-element.27), channel_id=1, source_target_pairs={{0,5},{1,6},{2,7},{3,0},{4,1},{5,2},{6,3},{7,4},{8,13},{9,14},{10,... | collective-permute-start | bytes 393224 | tf_op jit(solution)/shard_map/ppermute | solution.py:428
  84.5 1.6 %collective-permute-done.refs_1_ = bf16[4,128,128]{2,1,0:T(8,128)(2,1)S(1)} collective-permute-done((bf16[4,128,128]{2,1,0:T(8,128)(2,1)}, bf16[4,128,128]{2,1,0:T(8,128)(2,1)S(1)}, u32[]{:S(2)}, u32[]{:S(2)}) %collective-permute-start) | collective-permute-done | bytes 131104 | tf_op jit(solution)/shard_map/ppermute | solution.py:428
  86.1 4.1 %collective-permute-start.5 = (bf16[4,128,128]{2,1,0:T(8,128)(2,1)}, bf16[4,128,128]{2,1,0:T(8,128)(2,1)S(1)}, u32[]{:S(2)}, u32[]{:S(2)}) collective-permute-start(bf16[4,128,128]{2,1,0:T(8,128)(2,1)} %get-tuple-element.28), channel_id=1, source_target_pairs={{0,6},{1,7},{2,0},{3,1},{4,2},{5,3},{6,4},{7,5},{8,14},{9,15},{10,... | collective-permute-start | bytes 393224 | tf_op jit(solution)/shard_map/ppermute | solution.py:428
  90.2 2.8 %collective-permute-done.1.refs_2_ = bf16[4,128,128]{2,1,0:T(8,128)(2,1)S(1)} collective-permute-done((bf16[4,128,128]{2,1,0:T(8,128)(2,1)}, bf16[4,128,128]{2,1,0:T(8,128)(2,1)S(1)}, u32[]{:S(2)}, u32[]{:S(2)}) %collective-permute-start.1) | collective-permute-done | bytes 131104 | tf_op jit(solution)/shard_map/ppermute | solution.py:428
  93.0 2.2 %collective-permute-start.6 = (bf16[4,128,128]{2,1,0:T(8,128)(2,1)}, bf16[4,128,128]{2,1,0:T(8,128)(2,1)S(1)}, u32[]{:S(2)}, u32[]{:S(2)}) collective-permute-start(bf16[4,128,128]{2,1,0:T(8,128)(2,1)} %get-tuple-element.29), channel_id=1, source_target_pairs={{0,7},{1,0},{2,1},{3,2},{4,3},{5,4},{6,5},{7,6},{8,15},{9,8},{10,9... | collective-permute-start | bytes 393224 | tf_op jit(solution)/shard_map/ppermute | solution.py:428
  95.2 5.3 %collective-permute-done.2.refs_3_ = bf16[4,128,128]{2,1,0:T(8,128)(2,1)S(1)} collective-permute-done((bf16[4,128,128]{2,1,0:T(8,128)(2,1)}, bf16[4,128,128]{2,1,0:T(8,128)(2,1)S(1)}, u32[]{:S(2)}, u32[]{:S(2)}) %collective-permute-start.2) | collective-permute-done | bytes 131104 | tf_op jit(solution)/shard_map/ppermute | solution.py:428
  100.4 3.6 %collective-permute-done.3.refs_4_ = bf16[4,128,128]{2,1,0:T(8,128)(2,1)S(1)} collective-permute-done((bf16[4,128,128]{2,1,0:T(8,128)(2,1)}, bf16[4,128,128]{2,1,0:T(8,128)(2,1)S(1)}, u32[]{:S(2)}, u32[]{:S(2)}) %collective-permute-start.3) | collective-permute-done | bytes 131104 | tf_op jit(solution)/shard_map/ppermute | solution.py:428
  104.0 0.0 collective-permute-done.4.refs_5_
  104.0 0.0 collective-permute-done.5.refs_6_
  104.0 0.7 collective-permute-done.6.refs_7_
  104.8 0.9 copy-done
  105.7 0.1 join.1.x_ref
  105.7 0.6 rims.2
  106.3 1.9 %collective-permute-start.7 = (bf16[12,128,128]{2,1,0:T(8,128)(2,1)S(1)}, bf16[12,128,128]{2,1,0:T(8,128)(2,1)S(1)}, u32[]{:S(2)}, u32[]{:S(2)}) collective-permute-start(bf16[12,128,128]{2,1,0:T(8,128)(2,1)S(1)} %get-tuple-element.30), channel_id=1, source_target_pairs={{0,8},{16,24},{32,40},{48,56},{64,72},{80,88},{96,104},{112,120},{... | collective-permute-start | bytes 1179656 | tf_op jit(solution)/shard_map/ppermute | solution.py:419
  108.3 2.1 %collective-permute-start.8 = (bf16[12,128,128]{2,1,0:T(8,128)(2,1)S(1)}, bf16[12,128,128]{2,1,0:T(8,128)(2,1)S(1)}, u32[]{:S(2)}, u32[]{:S(2)}) collective-permute-start(bf16[12,128,128]{2,1,0:T(8,128)(2,1)S(1)} %get-tuple-element.31), channel_id=1, source_target_pairs={{8,16},{24,32},{40,48},{56,64},{72,80},{88,96},{104,112},{120,128}... | collective-permute-start | bytes 1179656 | tf_op jit(solution)/shard_map/ppermute | solution.py:419
  110.4 3.3 %inner.2 = (bf16[4,128,128]{2,1,0:T(8,128)(2,1)S(1)}, f32[2,1024,128]{2,1,0:T(8,128)S(1)}) custom-call(f32[61]{0:T(128)S(1)} %gate.1.info_ref.bias_ref, bf16[8,4,128,128]{3,2,1,0:T(8,128)(2,1)S(1)} %join.1.x_ref), custom_call_target="tpu_custom_call" | custom-call | flops 419430400 | bytes 5242880 | tf_op jit(solution)/shard_map/inner/pallas_call | solution.py:284
  113.7 0.0 collective-permute-done.7.first_ref
  113.7 5.8 %collective-permute-done.8.second_ref = bf16[12,128,128]{2,1,0:T(8,128)(2,1)S(1)} collective-permute-done((bf16[12,128,128]{2,1,0:T(8,128)(2,1)S(1)}, bf16[12,128,128]{2,1,0:T(8,128)(2,1)S(1)}, u32[]{:S(2)}, u32[]{:S(2)}) %collective-permute-start.8) | collective-permute-done | bytes 393248 | tf_op jit(solution)/shard_map/ppermute | solution.py:419
  119.5 5.7 %outer.2 = bf16[8,3,128,128]{3,2,1,0:T(8,128)(2,1)} custom-call(f32[61]{0:T(128)S(1)} %gate.1.info_ref.bias_ref, bf16[8,4,128,128]{3,2,1,0:T(8,128)(2,1)S(1)} %join.1.x_ref, bf16[12,128,128]{2,1,0:T(8,128)(2,1)S(1)} %collective-permute-done.7.first_ref, bf16[12,128,128]{2,1,0:T(8,128)(2,1)S(1)} %collective-permute-done.8.second_ref, ...), custom_call_target="tpu_custom_call" | custom-call | flops 671088640 | bytes 6291456 | tf_op jit(solution)/shard_map/outer/pallas_call | solution.py:366
  125.2 0.0 all-to-all-done.2.in_ref
  125.2 4.9 %all-to-all-start = ((bf16[8,3,128,128]{3,2,1,0:T(8,128)(2,1)}), bf16[8,3,128,128]{3,2,1,0:T(8,128)(2,1)S(1)}, u32[]{:S(2)}, u32[]{:S(2)}) async-start(bf16[8,3,128,128]{3,2,1,0:T(8,128)(2,1)} %outer.2), calls=%async_computation | async-start | bytes 1572864 | tf_op jit(solution)/shard_map/all_to_all | solution.py:415
  130.2 1.1 unpack.2
  131.2 21.2 %all-to-all-done.in_ref = bf16[8,3,128,128]{3,2,1,0:T(8,128)(2,1)S(1)} async-done(((bf16[8,3,128,128]{3,2,1,0:T(8,128)(2,1)}), bf16[8,3,128,128]{3,2,1,0:T(8,128)(2,1)S(1)}, u32[]{:S(2)}, u32[]{:S(2)}) %all-to-all-start) | async-done | bytes 786464 | tf_op jit(solution)/shard_map/all_to_all | solution.py:415
  152.5 1.1 unpack.3
  (9 shorter events, 0.1 us)
Async XLA Ops:
  2.9 36.0 %all-to-all-start.1 = ((bf16[8,4,128,128]{3,2,1,0:T(8,128)(2,1)}), bf16[8,4,128,128]{3,2,1,0:T(8,128)(2,1)S(1)}, u32[]{:S(2)}, u32[]{:S(2)}) async-start(bf16[8,4,128,128]{3,2,1,0:T(8,128)(2,1)} %pack.1), calls=%async_computation.1 | async-start | bytes 2097152 | tf_op jit(solution)/shard_map/all_to_all | solution.py:415
  9.7 0.7 copy-start.2
  9.7 0.7 copy-start.1
  39.5 7.6 %collective-permute-start.9 = (bf16[12,128,128]{2,1,0:T(8,128)(2,1)S(1)}, bf16[12,128,128]{2,1,0:T(8,128)(2,1)S(1)}, u32[]{:S(2)}, u32[]{:S(2)}) collective-permute-start(bf16[12,128,128]{2,1,0:T(8,128)(2,1)S(1)} %get-tuple-element.34), channel_id=1, source_target_pairs={{0,8},{16,24},{32,40},{48,56},{64,72},{80,88},{96,104},{112,120},{... | collective-permute-start | bytes 1179656 | tf_op jit(solution)/shard_map/ppermute | solution.py:419
  41.9 11.2 %collective-permute-start.10 = (bf16[12,128,128]{2,1,0:T(8,128)(2,1)S(1)}, bf16[12,128,128]{2,1,0:T(8,128)(2,1)S(1)}, u32[]{:S(2)}, u32[]{:S(2)}) collective-permute-start(bf16[12,128,128]{2,1,0:T(8,128)(2,1)S(1)} %get-tuple-element.35), channel_id=1, source_target_pairs={{8,16},{24,32},{40,48},{56,64},{72,80},{88,96},{104,112},{120,128}... | collective-permute-start | bytes 1179656 | tf_op jit(solution)/shard_map/ppermute | solution.py:419
  58.8 66.4 %all-to-all-start.2 = ((bf16[8,3,128,128]{3,2,1,0:T(8,128)(2,1)}), bf16[8,3,128,128]{3,2,1,0:T(8,128)(2,1)S(1)}, u32[]{:S(2)}, u32[]{:S(2)}) async-start(bf16[8,3,128,128]{3,2,1,0:T(8,128)(2,1)} %outer.3), calls=%async_computation.2 | async-start | bytes 1572864 | tf_op jit(solution)/shard_map/all_to_all | solution.py:415
  64.6 21.5 %collective-permute-start = (bf16[4,128,128]{2,1,0:T(8,128)(2,1)}, bf16[4,128,128]{2,1,0:T(8,128)(2,1)S(1)}, u32[]{:S(2)}, u32[]{:S(2)}) collective-permute-start(bf16[4,128,128]{2,1,0:T(8,128)(2,1)} %get-tuple-element.23), channel_id=1, source_target_pairs={{0,1},{1,2},{2,3},{3,4},{4,5},{5,6},{6,7},{7,0},{8,9},{9,10},{10,1... | collective-permute-start | bytes 393224 | tf_op jit(solution)/shard_map/ppermute | solution.py:428
  67.8 25.2 %collective-permute-start.1 = (bf16[4,128,128]{2,1,0:T(8,128)(2,1)}, bf16[4,128,128]{2,1,0:T(8,128)(2,1)S(1)}, u32[]{:S(2)}, u32[]{:S(2)}) collective-permute-start(bf16[4,128,128]{2,1,0:T(8,128)(2,1)} %get-tuple-element.24), channel_id=1, source_target_pairs={{0,2},{1,3},{2,4},{3,5},{4,6},{5,7},{6,0},{7,1},{8,10},{9,11},{10,... | collective-permute-start | bytes 393224 | tf_op jit(solution)/shard_map/ppermute | solution.py:428
  71.8 28.6 %collective-permute-start.2 = (bf16[4,128,128]{2,1,0:T(8,128)(2,1)}, bf16[4,128,128]{2,1,0:T(8,128)(2,1)S(1)}, u32[]{:S(2)}, u32[]{:S(2)}) collective-permute-start(bf16[4,128,128]{2,1,0:T(8,128)(2,1)} %get-tuple-element.25), channel_id=1, source_target_pairs={{0,3},{1,4},{2,5},{3,6},{4,7},{5,0},{6,1},{7,2},{8,11},{9,12},{10,... | collective-permute-start | bytes 393224 | tf_op jit(solution)/shard_map/ppermute | solution.py:428
  76.2 27.8 %collective-permute-start.3 = (bf16[4,128,128]{2,1,0:T(8,128)(2,1)}, bf16[4,128,128]{2,1,0:T(8,128)(2,1)S(1)}, u32[]{:S(2)}, u32[]{:S(2)}) collective-permute-start(bf16[4,128,128]{2,1,0:T(8,128)(2,1)} %get-tuple-element.26), channel_id=1, source_target_pairs={{0,4},{1,5},{2,6},{3,7},{4,0},{5,1},{6,2},{7,3},{8,12},{9,13},{10,... | collective-permute-start | bytes 393224 | tf_op jit(solution)/shard_map/ppermute | solution.py:428
  80.1 23.9 %collective-permute-start.4 = (bf16[4,128,128]{2,1,0:T(8,128)(2,1)}, bf16[4,128,128]{2,1,0:T(8,128)(2,1)S(1)}, u32[]{:S(2)}, u32[]{:S(2)}) collective-permute-start(bf16[4,128,128]{2,1,0:T(8,128)(2,1)} %get-tuple-element.27), channel_id=1, source_target_pairs={{0,5},{1,6},{2,7},{3,0},{4,1},{5,2},{6,3},{7,4},{8,13},{9,14},{10,... | collective-permute-start | bytes 393224 | tf_op jit(solution)/shard_map/ppermute | solution.py:428
  86.1 18.0 %collective-permute-start.5 = (bf16[4,128,128]{2,1,0:T(8,128)(2,1)}, bf16[4,128,128]{2,1,0:T(8,128)(2,1)S(1)}, u32[]{:S(2)}, u32[]{:S(2)}) collective-permute-start(bf16[4,128,128]{2,1,0:T(8,128)(2,1)} %get-tuple-element.28), channel_id=1, source_target_pairs={{0,6},{1,7},{2,0},{3,1},{4,2},{5,3},{6,4},{7,5},{8,14},{9,15},{10,... | collective-permute-start | bytes 393224 | tf_op jit(solution)/shard_map/ppermute | solution.py:428
  93.0 11.8 %collective-permute-start.6 = (bf16[4,128,128]{2,1,0:T(8,128)(2,1)}, bf16[4,128,128]{2,1,0:T(8,128)(2,1)S(1)}, u32[]{:S(2)}, u32[]{:S(2)}) collective-permute-start(bf16[4,128,128]{2,1,0:T(8,128)(2,1)} %get-tuple-element.29), channel_id=1, source_target_pairs={{0,7},{1,0},{2,1},{3,2},{4,3},{5,4},{6,5},{7,6},{8,15},{9,8},{10,9... | collective-permute-start | bytes 393224 | tf_op jit(solution)/shard_map/ppermute | solution.py:428
  104.7 0.9 copy-start
  106.3 7.3 %collective-permute-start.7 = (bf16[12,128,128]{2,1,0:T(8,128)(2,1)S(1)}, bf16[12,128,128]{2,1,0:T(8,128)(2,1)S(1)}, u32[]{:S(2)}, u32[]{:S(2)}) collective-permute-start(bf16[12,128,128]{2,1,0:T(8,128)(2,1)S(1)} %get-tuple-element.30), channel_id=1, source_target_pairs={{0,8},{16,24},{32,40},{48,56},{64,72},{80,88},{96,104},{112,120},{... | collective-permute-start | bytes 1179656 | tf_op jit(solution)/shard_map/ppermute | solution.py:419
  108.3 11.2 %collective-permute-start.8 = (bf16[12,128,128]{2,1,0:T(8,128)(2,1)S(1)}, bf16[12,128,128]{2,1,0:T(8,128)(2,1)S(1)}, u32[]{:S(2)}, u32[]{:S(2)}) collective-permute-start(bf16[12,128,128]{2,1,0:T(8,128)(2,1)S(1)} %get-tuple-element.31), channel_id=1, source_target_pairs={{8,16},{24,32},{40,48},{56,64},{72,80},{88,96},{104,112},{120,128}... | collective-permute-start | bytes 1179656 | tf_op jit(solution)/shard_map/ppermute | solution.py:419
  125.2 27.3 %all-to-all-start = ((bf16[8,3,128,128]{3,2,1,0:T(8,128)(2,1)}), bf16[8,3,128,128]{3,2,1,0:T(8,128)(2,1)S(1)}, u32[]{:S(2)}, u32[]{:S(2)}) async-start(bf16[8,3,128,128]{3,2,1,0:T(8,128)(2,1)} %outer.2), calls=%async_computation | async-start | bytes 1572864 | tf_op jit(solution)/shard_map/all_to_all | solution.py:415

commit v5 on v4

--- a/solution.py
+++ b/solution.py
@@ -1,3 +1,5 @@
+import functools
+
 import jax
 import jax.numpy as jnp
 from jax import lax
@@ -14,6 +16,7 @@
 SPAN = WINDOW * TILE
 SCALE = float(HEAD_DIM) ** (-0.5)
 CHUNKS = 2
+LAUNCH = 16
 ORDER = (4, 3, 5, 2, 6, 1, 7)
 VMEM = pl.BlockSpec(memory_space=pltpu.VMEM)
 NT = (((1,), (1,)), ((), ()))
@@ -232,7 +235,11 @@
     return (jnp.where(first, both[:TILE], both[TILE:]) * SCALE).astype(jnp.bfloat16)
 
 
-def inner_body(bias_ref, x_ref, dquery_ref, edge_ref, key_ref, value_ref, *held):
+def inner_body(ahead, bias_ref, *refs):
+    pl.when((bias_ref[bias_ref.shape[0] - 2] > 0.5) == ahead)(lambda: inner_work(bias_ref, *refs))
+
+
+def inner_work(bias_ref, x_ref, dquery_ref, edge_ref, key_ref, value_ref, *held):
     tiles = x_ref.shape[0]
     held = (held[:6], held[6:])
     for t in range(tiles):
@@ -277,12 +284,12 @@
     end(steps - 1, 1)
 
 
-def inner(bias, taken):
+def inner(bias, taken, ahead):
     tiles = taken.shape[0]
     steps = tiles - 2 * REACH
     whole = tiles * TILE
     return pl.pallas_call(
-        inner_body,
+        functools.partial(inner_body, ahead),
         in_specs=[pl.BlockSpec(memory_space=pltpu.SMEM), VMEM],
         out_specs=[VMEM] * 2,
         out_shape=[
@@ -297,7 +304,7 @@
 
 
 def outer_body(
-    bias_ref, x_ref, first_ref, second_ref, dquery_ref, edge_ref, out_ref, halo_ref, key_ref, value_ref, acc_ref, *held
+    bias_ref, x_ref, first_ref, second_ref, dquery0_ref, edge0_ref, dquery1_ref, edge1_ref, out_ref, halo_ref, key_ref, value_ref, acc_ref, *held
 ):
     tiles = x_ref.shape[0]
     deep = 2 * REACH
@@ -312,9 +319,15 @@
             ref[(deep + t) * TILE:(deep + t + 1) * TILE] = x_ref[t, n]
             ref[(2 * deep + t) * TILE:(2 * deep + t + 1) * TILE] = x_ref[tiles - deep + t, n]
             ref[(3 * deep + t) * TILE:(3 * deep + t + 1) * TILE] = high_ref[(n - 1) * deep + t]
-    acc_ref[...] = edge_ref[...]
-    for t in range(tiles - 2 * REACH):
-        out_ref[REACH + t, 0] = dquery_ref[t]
+    ahead = bias_ref[bias_ref.shape[0] - 2] > 0.5
+
+    def adopt(dquery_ref, edge_ref):
+        acc_ref[...] = edge_ref[...]
+        for t in range(tiles - 2 * REACH):
+            out_ref[REACH + t, 0] = dquery_ref[t]
+
+    pl.when(ahead)(lambda: adopt(dquery0_ref, edge0_ref))
+    pl.when(jnp.logical_not(ahead))(lambda: adopt(dquery1_ref, edge1_ref))
 
     def place(step):
         j, high = step // 2, step % 2 == 1
@@ -360,22 +373,22 @@
             out_ref[tile, 1 + n] = acc_ref[n, t * TILE:(t + 1) * TILE].astype(jnp.bfloat16)
 
 
-def outer(bias, taken, first, second, dquery, edge):
+def outer(bias, taken, first, second, *parts):
     tiles = taken.shape[0]
     steps = 4 * REACH
     return pl.pallas_call(
         outer_body,
-        in_specs=[pl.BlockSpec(memory_space=pltpu.SMEM)] + [VMEM] * 5,
+        in_specs=[pl.BlockSpec(memory_space=pltpu.SMEM)] + [VMEM] * 7,
         out_specs=VMEM,
         out_shape=jax.ShapeDtypeStruct((tiles, 3, TILE, LANES), jnp.bfloat16),
         scratch_shapes=[pltpu.VMEM((2,) + first.shape, jnp.bfloat16)]
         + [pltpu.VMEM((8 * REACH * TILE, LANES), jnp.bfloat16)] * 2
-        + [pltpu.VMEM(edge.shape, jnp.float32)]
+        + [pltpu.VMEM(parts[1].shape, jnp.float32)]
         + held_shapes() * 2,
         compiler_params=pltpu.CompilerParams(vmem_limit_bytes=28 << 20),
         cost_estimate=cost(steps * WINDOW * 8 * TILE * TILE * LANES, 6 << 20, steps * WINDOW * 2 * TILE * TILE),
         name="outer",
-    )(bias, taken, first, second, dquery, edge)
+    )(bias, taken, first, second, *parts)
 
 
 def tile_bias(near_mask, motion_count, first, tiles):
@@ -387,8 +400,10 @@
     index = first - REACH + jnp.arange(tiles + 2 * REACH)
     others = index[:, None] + jnp.arange(-REACH, REACH + 1)[None, :]
     allowed &= (others >= 0) & (others < total)
-    odd = (first // tiles % 2).astype(jnp.float32)
-    return jnp.concatenate([jnp.where(allowed, 0.0, -1e30).astype(jnp.float32).reshape(-1), odd[None]])
+    group = first // tiles
+    ahead = ((group > 0) & (group % LAUNCH == 0)).astype(jnp.float32)
+    odd = (group % 2).astype(jnp.float32)
+    return jnp.concatenate([jnp.where(allowed, 0.0, -1e30).astype(jnp.float32).reshape(-1), ahead[None], odd[None]])
 
 
 def gate(table):
@@ -430,9 +445,10 @@
     info = gate(bias)
     for c in range(CHUNKS):
         first, second = rims(info, taken[c])
+        parts = inner(info, taken[c], True)
+        second = swap(second, 1)
         first = swap(first, 0)
-        second = swap(second, 1)
-        parts = inner(info, taken[c])
+        parts += inner(info, taken[c], False)
         out = outer(info, taken[c], first, second, *parts)
         back = exchange(out)
         results = unpack(back, c, columns, results)

time: 155 us -> 155 us (level)
  the two profiles are of different devices: /device:TPU:449 before, /device:TPU:4 now
where the time goes in v5:
time: 155 us; the launch traced here: 154 us
  starting transfers between devices  70.4 us (45%)
  waiting for transfers between devices  53.6 us (35%)
  Pallas kernels  27.3 us (18%)
  local copies, waits for them, and re-layouts  1.77 us (1%)
    all_to_all x3, waiting for transfers between devices, exchange(): return lax.all_to_all(x, 'blk', split_axis=0, concat_axis=0, tiled=True)  44.3 us
    ppermute x7, starting transfers between devices, per_device(): lax.ppermute(blocks[n], 'blk', [(i, (i + n) % tiles) for i in range(tiles)])  30.2 us
    ppermute x4, starting transfers between devices, swap(): return lax.ppermute(x, 'seq', right + [(j, i) for i, j in right])  24.3 us
    all_to_all x3, starting transfers between devices, exchange(): return lax.all_to_all(x, 'blk', split_axis=0, concat_axis=0, tiled=True)  15.9 us
    pallas_call x2, Pallas kernels, outer(): pl.pallas_call(outer_body, in_specs=[pl.BlockSpec(memory_space=pltpu.SMEM...  11.6 us
    pallas_call x4, Pallas kernels, inner(): pl.pallas_call(functools.partial(inner_body, ahead), in_specs=[pl.BlockSp...  7.83 us
    ppermute x7, waiting for transfers between devices, per_device(): lax.ppermute(blocks[n], 'blk', [(i, (i + n) % tiles) for i in range(tiles)])  6.25 us
  transfers between devices with their start and end apart: 14, of which 9 were waited for; matrix products, arithmetic and copies ran while one was open for 0% of the time, Pallas kernels for 11%

profile of v5, /device:TPU:4, one launch (start us, length us, event | category | flops | bytes accessed | tf_op | source)
XLA Modules:
  0.0 154.4 jit_solution(15937646868973859211)
XLA Ops:
  0.6 2.2 %pack.1 = bf16[8,4,128,128]{3,2,1,0:T(8,128)(2,1)} custom-call(bf16[128,2048]{1,0:T(8,128)(2,1)} %refs_0_.3, bf16[128,2048]{1,0:T(8,128)(2,1)} %refs_1_.3, bf16[128,2048]{1,0:T(8,128)(2,1)} %refs_2_.3, bf16[128,2048]{1,0:T(8,128)(2,1)} %refs_3_.3), custom_call_target="tpu_custom_call" | custom-call | bytes 2097152 | tf_op jit(solution)/shard_map/pack/pallas_call | solution.py:56
  2.9 7.1 %all-to-all-start.1 = ((bf16[8,4,128,128]{3,2,1,0:T(8,128)(2,1)}), bf16[8,4,128,128]{3,2,1,0:T(8,128)(2,1)S(1)}, u32[]{:S(2)}, u32[]{:S(2)}) async-start(bf16[8,4,128,128]{3,2,1,0:T(8,128)(2,1)} %pack.1), calls=%async_computation.1 | async-start | bytes 2097152 | tf_op jit(solution)/shard_map/all_to_all | solution.py:430
  10.0 0.0 copy-start.1
  10.0 0.6 copy-done.2
  10.7 0.1 compare_bitcast_fusion
  10.8 0.1 fusion.3
  10.9 0.1 fusion.2
  11.0 0.1 copy.13
  11.1 0.1 reshape.31
  11.2 0.1 pad_maximum_fusion.in_ref
  11.2 27.5 %all-to-all-done.1.x_ref.refs_0_ = bf16[8,4,128,128]{3,2,1,0:T(8,128)(2,1)S(1)} async-done(((bf16[8,4,128,128]{3,2,1,0:T(8,128)(2,1)}), bf16[8,4,128,128]{3,2,1,0:T(8,128)(2,1)S(1)}, u32[]{:S(2)}, u32[]{:S(2)}) %all-to-all-start.1) | async-done | bytes 1048608 | tf_op jit(solution)/shard_map/all_to_all | solution.py:430
  38.7 0.6 rims.3
  39.3 1.9 %collective-permute-start.9 = (bf16[12,128,128]{2,1,0:T(8,128)(2,1)S(1)}, bf16[12,128,128]{2,1,0:T(8,128)(2,1)S(1)}, u32[]{:S(2)}, u32[]{:S(2)}) collective-permute-start(bf16[12,128,128]{2,1,0:T(8,128)(2,1)S(1)} %get-tuple-element.40), channel_id=1, source_target_pairs={{0,8},{16,24},{32,40},{48,56},{64,72},{80,88},{96,104},{112,120},{... | collective-permute-start | bytes 1179656 | tf_op jit(solution)/shard_map/ppermute | solution.py:434
  41.3 11.0 %collective-permute-start.10 = (bf16[12,128,128]{2,1,0:T(8,128)(2,1)S(1)}, bf16[12,128,128]{2,1,0:T(8,128)(2,1)S(1)}, u32[]{:S(2)}, u32[]{:S(2)}) collective-permute-start(bf16[12,128,128]{2,1,0:T(8,128)(2,1)S(1)} %get-tuple-element.41), channel_id=1, source_target_pairs={{8,16},{24,32},{40,48},{56,64},{72,80},{88,96},{104,112},{120,128}... | collective-permute-start | bytes 1179656 | tf_op jit(solution)/shard_map/ppermute | solution.py:434
  52.3 3.3 %inner.6 = (bf16[4,128,128]{2,1,0:T(8,128)(2,1)S(1)}, f32[2,1024,128]{2,1,0:T(8,128)S(1)}) custom-call(f32[62]{0:T(128)S(1)} %gate.1.info_ref.bias_ref, bf16[8,4,128,128]{3,2,1,0:T(8,128)(2,1)S(1)} %all-to-all-done.1.x_ref.refs_0_), custom_call_target="tpu_custom_call" | custom-call | flops 419430400 | bytes 5242880 | tf_op jit(solution)/shard_map/inner/pallas_call | solution.py:291
  55.6 0.5 inner.7
  56.1 1.6 %collective-permute-done.10.second_ref = bf16[12,128,128]{2,1,0:T(8,128)(2,1)S(1)} collective-permute-done((bf16[12,128,128]{2,1,0:T(8,128)(2,1)S(1)}, bf16[12,128,128]{2,1,0:T(8,128)(2,1)S(1)}, u32[]{:S(2)}, u32[]{:S(2)}) %collective-permute-start.10) | collective-permute-done | bytes 393248 | tf_op jit(solution)/shard_map/ppermute | solution.py:434
  57.7 5.8 %outer.3 = bf16[8,3,128,128]{3,2,1,0:T(8,128)(2,1)} custom-call(f32[62]{0:T(128)S(1)} %gate.1.info_ref.bias_ref, bf16[8,4,128,128]{3,2,1,0:T(8,128)(2,1)S(1)} %all-to-all-done.1.x_ref.refs_0_, bf16[12,128,128]{2,1,0:T(8,128)(2,1)S(1)} %collective-permute-done.9.first_ref, bf16[12,128,128]{2,1,0:T(8,128)(2,1)S(1)} %collective-permute-done.10.second_ref, ...), custom_call_target="tpu_custom_call" | custom-call | flops 671088640 | bytes 6291456 | tf_op jit(solution)/shard_map/outer/pallas_call | solution.py:379
  63.5 3.5 %all-to-all-start.2 = ((bf16[8,3,128,128]{3,2,1,0:T(8,128)(2,1)}), bf16[8,3,128,128]{3,2,1,0:T(8,128)(2,1)S(1)}, u32[]{:S(2)}, u32[]{:S(2)}) async-start(bf16[8,3,128,128]{3,2,1,0:T(8,128)(2,1)} %outer.3), calls=%async_computation.2 | async-start | bytes 1572864 | tf_op jit(solution)/shard_map/all_to_all | solution.py:430
  67.1 2.2 %pack_around.1 = (bf16[4,128,128]{2,1,0:T(8,128)(2,1)}, bf16[4,128,128]{2,1,0:T(8,128)(2,1)}, bf16[4,128,128]{2,1,0:T(8,128)(2,1)}, bf16[4,128,128]{2,1,0:T(8,12...) custom-call(s32[1]{0:T(128)} %bitcast.3.me_ref, ...), custom_call_target="tpu_custom_call" | custom-call | bytes 2097152 | tf_op jit(solution)/shard_map/pack_around/pallas_call | solution.py:97
  69.3 3.8 %collective-permute-start = (bf16[4,128,128]{2,1,0:T(8,128)(2,1)}, bf16[4,128,128]{2,1,0:T(8,128)(2,1)S(1)}, u32[]{:S(2)}, u32[]{:S(2)}) collective-permute-start(bf16[4,128,128]{2,1,0:T(8,128)(2,1)} %get-tuple-element.27), channel_id=1, source_target_pairs={{0,1},{1,2},{2,3},{3,4},{4,5},{5,6},{6,7},{7,0},{8,9},{9,10},{10,1... | collective-permute-start | bytes 393224 | tf_op jit(solution)/shard_map/ppermute | solution.py:443
  73.1 4.3 %collective-permute-start.1 = (bf16[4,128,128]{2,1,0:T(8,128)(2,1)}, bf16[4,128,128]{2,1,0:T(8,128)(2,1)S(1)}, u32[]{:S(2)}, u32[]{:S(2)}) collective-permute-start(bf16[4,128,128]{2,1,0:T(8,128)(2,1)} %get-tuple-element.28), channel_id=1, source_target_pairs={{0,2},{1,3},{2,4},{3,5},{4,6},{5,7},{6,0},{7,1},{8,10},{9,11},{10,... | collective-permute-start | bytes 393224 | tf_op jit(solution)/shard_map/ppermute | solution.py:443
  77.4 4.6 %collective-permute-start.2 = (bf16[4,128,128]{2,1,0:T(8,128)(2,1)}, bf16[4,128,128]{2,1,0:T(8,128)(2,1)S(1)}, u32[]{:S(2)}, u32[]{:S(2)}) collective-permute-start(bf16[4,128,128]{2,1,0:T(8,128)(2,1)} %get-tuple-element.29), channel_id=1, source_target_pairs={{0,3},{1,4},{2,5},{3,6},{4,7},{5,0},{6,1},{7,2},{8,11},{9,12},{10,... | collective-permute-start | bytes 393224 | tf_op jit(solution)/shard_map/ppermute | solution.py:443
  82.0 4.2 %collective-permute-start.3 = (bf16[4,128,128]{2,1,0:T(8,128)(2,1)}, bf16[4,128,128]{2,1,0:T(8,128)(2,1)S(1)}, u32[]{:S(2)}, u32[]{:S(2)}) collective-permute-start(bf16[4,128,128]{2,1,0:T(8,128)(2,1)} %get-tuple-element.30), channel_id=1, source_target_pairs={{0,4},{1,5},{2,6},{3,7},{4,0},{5,1},{6,2},{7,3},{8,12},{9,13},{10,... | collective-permute-start | bytes 393224 | tf_op jit(solution)/shard_map/ppermute | solution.py:443
  86.3 4.6 %collective-permute-start.4 = (bf16[4,128,128]{2,1,0:T(8,128)(2,1)}, bf16[4,128,128]{2,1,0:T(8,128)(2,1)S(1)}, u32[]{:S(2)}, u32[]{:S(2)}) collective-permute-start(bf16[4,128,128]{2,1,0:T(8,128)(2,1)} %get-tuple-element.31), channel_id=1, source_target_pairs={{0,5},{1,6},{2,7},{3,0},{4,1},{5,2},{6,3},{7,4},{8,13},{9,14},{10,... | collective-permute-start | bytes 393224 | tf_op jit(solution)/shard_map/ppermute | solution.py:443
  90.9 1.2 collective-permute-done.refs_1_
  92.1 4.9 %collective-permute-start.5 = (bf16[4,128,128]{2,1,0:T(8,128)(2,1)}, bf16[4,128,128]{2,1,0:T(8,128)(2,1)S(1)}, u32[]{:S(2)}, u32[]{:S(2)}) collective-permute-start(bf16[4,128,128]{2,1,0:T(8,128)(2,1)} %get-tuple-element.32), channel_id=1, source_target_pairs={{0,6},{1,7},{2,0},{3,1},{4,2},{5,3},{6,4},{7,5},{8,14},{9,15},{10,... | collective-permute-start | bytes 393224 | tf_op jit(solution)/shard_map/ppermute | solution.py:443
  97.0 0.2 collective-permute-done.1.refs_2_
  97.2 3.7 %collective-permute-start.6 = (bf16[4,128,128]{2,1,0:T(8,128)(2,1)}, bf16[4,128,128]{2,1,0:T(8,128)(2,1)S(1)}, u32[]{:S(2)}, u32[]{:S(2)}) collective-permute-start(bf16[4,128,128]{2,1,0:T(8,128)(2,1)} %get-tuple-element.33), channel_id=1, source_target_pairs={{0,7},{1,0},{2,1},{3,2},{4,3},{5,4},{6,5},{7,6},{8,15},{9,8},{10,9... | collective-permute-start | bytes 393224 | tf_op jit(solution)/shard_map/ppermute | solution.py:443
  100.9 1.4 collective-permute-done.2.refs_3_
  102.3 2.0 %collective-permute-done.3.refs_4_ = bf16[4,128,128]{2,1,0:T(8,128)(2,1)S(1)} collective-permute-done((bf16[4,128,128]{2,1,0:T(8,128)(2,1)}, bf16[4,128,128]{2,1,0:T(8,128)(2,1)S(1)}, u32[]{:S(2)}, u32[]{:S(2)}) %collective-permute-start.3) | collective-permute-done | bytes 131104 | tf_op jit(solution)/shard_map/ppermute | solution.py:443
  104.4 0.0 collective-permute-done.4.refs_5_
  104.4 0.0 collective-permute-done.5.refs_6_
  104.4 1.4 collective-permute-done.6.refs_7_
  105.8 0.9 copy-done
  106.7 0.1 join.1.x_ref.refs_0_
  106.7 0.6 rims.2
  107.4 1.9 %collective-permute-start.7 = (bf16[12,128,128]{2,1,0:T(8,128)(2,1)S(1)}, bf16[12,128,128]{2,1,0:T(8,128)(2,1)S(1)}, u32[]{:S(2)}, u32[]{:S(2)}) collective-permute-start(bf16[12,128,128]{2,1,0:T(8,128)(2,1)S(1)} %get-tuple-element.34), channel_id=1, source_target_pairs={{0,8},{16,24},{32,40},{48,56},{64,72},{80,88},{96,104},{112,120},{... | collective-permute-start | bytes 1179656 | tf_op jit(solution)/shard_map/ppermute | solution.py:434
  109.3 9.5 %collective-permute-start.8 = (bf16[12,128,128]{2,1,0:T(8,128)(2,1)S(1)}, bf16[12,128,128]{2,1,0:T(8,128)(2,1)S(1)}, u32[]{:S(2)}, u32[]{:S(2)}) collective-permute-start(bf16[12,128,128]{2,1,0:T(8,128)(2,1)S(1)} %get-tuple-element.35), channel_id=1, source_target_pairs={{8,16},{24,32},{40,48},{56,64},{72,80},{88,96},{104,112},{120,128}... | collective-permute-start | bytes 1179656 | tf_op jit(solution)/shard_map/ppermute | solution.py:434
  118.7 3.5 %inner.4 = (bf16[4,128,128]{2,1,0:T(8,128)(2,1)S(1)}, f32[2,1024,128]{2,1,0:T(8,128)S(1)}) custom-call(f32[62]{0:T(128)S(1)} %gate.1.info_ref.bias_ref, bf16[8,4,128,128]{3,2,1,0:T(8,128)(2,1)S(1)} %join.1.x_ref.refs_0_), custom_call_target="tpu_custom_call" | custom-call | flops 419430400 | bytes 5242880 | tf_op jit(solution)/shard_map/inner/pallas_call | solution.py:291
  122.2 0.5 inner.5
  122.8 0.0 collective-permute-done.7.first_ref
  122.8 1.4 collective-permute-done.8.second_ref
  124.2 5.8 %outer.2 = bf16[8,3,128,128]{3,2,1,0:T(8,128)(2,1)} custom-call(f32[62]{0:T(128)S(1)} %gate.1.info_ref.bias_ref, bf16[8,4,128,128]{3,2,1,0:T(8,128)(2,1)S(1)} %join.1.x_ref.refs_0_, bf16[12,128,128]{2,1,0:T(8,128)(2,1)S(1)} %collective-permute-done.7.first_ref, bf16[12,128,128]{2,1,0:T(8,128)(2,1)S(1)} %collective-permute-done.8.second_ref, ...), custom_call_target="tpu_custom_call" | custom-call | flops 671088640 | bytes 6291456 | tf_op jit(solution)/shard_map/outer/pallas_call | solution.py:379
  130.0 5.2 %all-to-all-start = ((bf16[8,3,128,128]{3,2,1,0:T(8,128)(2,1)}), bf16[8,3,128,128]{3,2,1,0:T(8,128)(2,1)S(1)}, u32[]{:S(2)}, u32[]{:S(2)}) async-start(bf16[8,3,128,128]{3,2,1,0:T(8,128)(2,1)} %outer.2), calls=%async_computation | async-start | bytes 1572864 | tf_op jit(solution)/shard_map/all_to_all | solution.py:430
  135.2 1.1 unpack.2
  136.3 16.8 %all-to-all-done.in_ref = bf16[8,3,128,128]{3,2,1,0:T(8,128)(2,1)S(1)} async-done(((bf16[8,3,128,128]{3,2,1,0:T(8,128)(2,1)}), bf16[8,3,128,128]{3,2,1,0:T(8,128)(2,1)S(1)}, u32[]{:S(2)}, u32[]{:S(2)}) %all-to-all-start) | async-done | bytes 786464 | tf_op jit(solution)/shard_map/all_to_all | solution.py:430
  153.1 1.1 unpack.3
  (11 shorter events, 0.1 us)
Async XLA Ops:
  2.9 35.8 %all-to-all-start.1 = ((bf16[8,4,128,128]{3,2,1,0:T(8,128)(2,1)}), bf16[8,4,128,128]{3,2,1,0:T(8,128)(2,1)S(1)}, u32[]{:S(2)}, u32[]{:S(2)}) async-start(bf16[8,4,128,128]{3,2,1,0:T(8,128)(2,1)} %pack.1), calls=%async_computation.1 | async-start | bytes 2097152 | tf_op jit(solution)/shard_map/all_to_all | solution.py:430
  10.0 0.7 copy-start.2
  10.0 0.7 copy-start.1
  39.3 16.8 %collective-permute-start.9 = (bf16[12,128,128]{2,1,0:T(8,128)(2,1)S(1)}, bf16[12,128,128]{2,1,0:T(8,128)(2,1)S(1)}, u32[]{:S(2)}, u32[]{:S(2)}) collective-permute-start(bf16[12,128,128]{2,1,0:T(8,128)(2,1)S(1)} %get-tuple-element.40), channel_id=1, source_target_pairs={{0,8},{16,24},{32,40},{48,56},{64,72},{80,88},{96,104},{112,120},{... | collective-permute-start | bytes 1179656 | tf_op jit(solution)/shard_map/ppermute | solution.py:434
  41.3 16.5 %collective-permute-start.10 = (bf16[12,128,128]{2,1,0:T(8,128)(2,1)S(1)}, bf16[12,128,128]{2,1,0:T(8,128)(2,1)S(1)}, u32[]{:S(2)}, u32[]{:S(2)}) collective-permute-start(bf16[12,128,128]{2,1,0:T(8,128)(2,1)S(1)} %get-tuple-element.41), channel_id=1, source_target_pairs={{8,16},{24,32},{40,48},{56,64},{72,80},{88,96},{104,112},{120,128}... | collective-permute-start | bytes 1179656 | tf_op jit(solution)/shard_map/ppermute | solution.py:434
  63.5 66.5 %all-to-all-start.2 = ((bf16[8,3,128,128]{3,2,1,0:T(8,128)(2,1)}), bf16[8,3,128,128]{3,2,1,0:T(8,128)(2,1)S(1)}, u32[]{:S(2)}, u32[]{:S(2)}) async-start(bf16[8,3,128,128]{3,2,1,0:T(8,128)(2,1)} %outer.3), calls=%async_computation.2 | async-start | bytes 1572864 | tf_op jit(solution)/shard_map/all_to_all | solution.py:430
  69.3 22.8 %collective-permute-start = (bf16[4,128,128]{2,1,0:T(8,128)(2,1)}, bf16[4,128,128]{2,1,0:T(8,128)(2,1)S(1)}, u32[]{:S(2)}, u32[]{:S(2)}) collective-permute-start(bf16[4,128,128]{2,1,0:T(8,128)(2,1)} %get-tuple-element.27), channel_id=1, source_target_pairs={{0,1},{1,2},{2,3},{3,4},{4,5},{5,6},{6,7},{7,0},{8,9},{9,10},{10,1... | collective-permute-start | bytes 393224 | tf_op jit(solution)/shard_map/ppermute | solution.py:443
  73.1 24.1 %collective-permute-start.1 = (bf16[4,128,128]{2,1,0:T(8,128)(2,1)}, bf16[4,128,128]{2,1,0:T(8,128)(2,1)S(1)}, u32[]{:S(2)}, u32[]{:S(2)}) collective-permute-start(bf16[4,128,128]{2,1,0:T(8,128)(2,1)} %get-tuple-element.28), channel_id=1, source_target_pairs={{0,2},{1,3},{2,4},{3,5},{4,6},{5,7},{6,0},{7,1},{8,10},{9,11},{10,... | collective-permute-start | bytes 393224 | tf_op jit(solution)/shard_map/ppermute | solution.py:443
  77.4 24.9 %collective-permute-start.2 = (bf16[4,128,128]{2,1,0:T(8,128)(2,1)}, bf16[4,128,128]{2,1,0:T(8,128)(2,1)S(1)}, u32[]{:S(2)}, u32[]{:S(2)}) collective-permute-start(bf16[4,128,128]{2,1,0:T(8,128)(2,1)} %get-tuple-element.29), channel_id=1, source_target_pairs={{0,3},{1,4},{2,5},{3,6},{4,7},{5,0},{6,1},{7,2},{8,11},{9,12},{10,... | collective-permute-start | bytes 393224 | tf_op jit(solution)/shard_map/ppermute | solution.py:443
  82.0 22.3 %collective-permute-start.3 = (bf16[4,128,128]{2,1,0:T(8,128)(2,1)}, bf16[4,128,128]{2,1,0:T(8,128)(2,1)S(1)}, u32[]{:S(2)}, u32[]{:S(2)}) collective-permute-start(bf16[4,128,128]{2,1,0:T(8,128)(2,1)} %get-tuple-element.30), channel_id=1, source_target_pairs={{0,4},{1,5},{2,6},{3,7},{4,0},{5,1},{6,2},{7,3},{8,12},{9,13},{10,... | collective-permute-start | bytes 393224 | tf_op jit(solution)/shard_map/ppermute | solution.py:443
  86.3 18.1 %collective-permute-start.4 = (bf16[4,128,128]{2,1,0:T(8,128)(2,1)}, bf16[4,128,128]{2,1,0:T(8,128)(2,1)S(1)}, u32[]{:S(2)}, u32[]{:S(2)}) collective-permute-start(bf16[4,128,128]{2,1,0:T(8,128)(2,1)} %get-tuple-element.31), channel_id=1, source_target_pairs={{0,5},{1,6},{2,7},{3,0},{4,1},{5,2},{6,3},{7,4},{8,13},{9,14},{10,... | collective-permute-start | bytes 393224 | tf_op jit(solution)/shard_map/ppermute | solution.py:443
  92.1 12.3 %collective-permute-start.5 = (bf16[4,128,128]{2,1,0:T(8,128)(2,1)}, bf16[4,128,128]{2,1,0:T(8,128)(2,1)S(1)}, u32[]{:S(2)}, u32[]{:S(2)}) collective-permute-start(bf16[4,128,128]{2,1,0:T(8,128)(2,1)} %get-tuple-element.32), channel_id=1, source_target_pairs={{0,6},{1,7},{2,0},{3,1},{4,2},{5,3},{6,4},{7,5},{8,14},{9,15},{10,... | collective-permute-start | bytes 393224 | tf_op jit(solution)/shard_map/ppermute | solution.py:443
  97.2 8.6 %collective-permute-start.6 = (bf16[4,128,128]{2,1,0:T(8,128)(2,1)}, bf16[4,128,128]{2,1,0:T(8,128)(2,1)S(1)}, u32[]{:S(2)}, u32[]{:S(2)}) collective-permute-start(bf16[4,128,128]{2,1,0:T(8,128)(2,1)} %get-tuple-element.33), channel_id=1, source_target_pairs={{0,7},{1,0},{2,1},{3,2},{4,3},{5,4},{6,5},{7,6},{8,15},{9,8},{10,9... | collective-permute-start | bytes 393224 | tf_op jit(solution)/shard_map/ppermute | solution.py:443
  105.8 0.9 copy-start
  107.4 15.4 %collective-permute-start.7 = (bf16[12,128,128]{2,1,0:T(8,128)(2,1)S(1)}, bf16[12,128,128]{2,1,0:T(8,128)(2,1)S(1)}, u32[]{:S(2)}, u32[]{:S(2)}) collective-permute-start(bf16[12,128,128]{2,1,0:T(8,128)(2,1)S(1)} %get-tuple-element.34), channel_id=1, source_target_pairs={{0,8},{16,24},{32,40},{48,56},{64,72},{80,88},{96,104},{112,120},{... | collective-permute-start | bytes 1179656 | tf_op jit(solution)/shard_map/ppermute | solution.py:434
  109.3 14.9 %collective-permute-start.8 = (bf16[12,128,128]{2,1,0:T(8,128)(2,1)S(1)}, bf16[12,128,128]{2,1,0:T(8,128)(2,1)S(1)}, u32[]{:S(2)}, u32[]{:S(2)}) collective-permute-start(bf16[12,128,128]{2,1,0:T(8,128)(2,1)S(1)} %get-tuple-element.35), channel_id=1, source_target_pairs={{8,16},{24,32},{40,48},{56,64},{72,80},{88,96},{104,112},{120,128}... | collective-permute-start | bytes 1179656 | tf_op jit(solution)/shard_map/ppermute | solution.py:434
  130.0 23.1 %all-to-all-start = ((bf16[8,3,128,128]{3,2,1,0:T(8,128)(2,1)}), bf16[8,3,128,128]{3,2,1,0:T(8,128)(2,1)S(1)}, u32[]{:S(2)}, u32[]{:S(2)}) async-start(bf16[8,3,128,128]{3,2,1,0:T(8,128)(2,1)} %outer.2), calls=%async_computation | async-start | bytes 1572864 | tf_op jit(solution)/shard_map/all_to_all | solution.py:430
